TPU v7x, 32 devices: a whole 2x2x4 slice. The times are simulated.
32 devices in a mesh: dp: 8 (over z, y), mp: 4 (over x, core).
Axes of the slice: x: 2, y: 2, z: 4, core: 2. Of those that a mesh axis runs over, the one named last changes fastest.
Arguments:
- latents: bfloat16 [262144, 256], P(('dp', 'mp')), may hold values from -6 to 6
- proj_weight: bfloat16 [18, 256], replicated, may hold values from -0.375 to 0.375
- proj_bias: float32 [18], replicated, may hold values from -2.5 to 2.5
- fill: int32 [2048], replicated, may hold values from 0 to 128, as said below
- target: int32 [2048], replicated, may hold values from -1 to 7, as said below
- target_slot: int32 [2048], replicated, may hold values from -1 to 31, as said below
Outputs:
- latent_grad: bfloat16 [131072, 256], P(('dp', 'mp'))
- weight_grad: float32 [18, 256], replicated
- entropy_loss: float32 [], replicated
Inputs may be any that keep to these rules, and one draw needn't show every extreme that they name: `fill`: zero exactly on the empty slots of a device, which are those whose target is -1. `target`: blocks go to devices with the same mp index. Each device receives exactly 32 blocks, one in each of its positions; at most 8 blocks goes from one device to any one index of dp, and some device does send 8 block to an index. -1 marks an empty slot. `target_slot`: -1 exactly where target is -1.
All inputs are finite; a program needn't handle non-finite values.
Results may differ from a plain program's by a relative error of at most 0.0049.
Values may be sent and summed in bfloat16 or wider, within the bound.
A program may use at most 64 MiB of HBM per device.

v0:
```python
import jax
import jax.numpy as jnp
from jax import lax
from jax.sharding import PartitionSpec as P

BLK = 128
OUT_SLOTS = 32


sharpness = 2.0


def routing(fill, target, target_slot, n_dp, n_mp, in_slots, capacity, own_dp, own_mp):
    col_shape = (n_dp, n_mp, in_slots)
    col_fill = lax.dynamic_index_in_dim(fill.reshape(col_shape), own_mp, 1, keepdims=False)
    col_target = lax.dynamic_index_in_dim(target.reshape(col_shape), own_mp, 1, keepdims=False)
    col_slot = lax.dynamic_index_in_dim(target_slot.reshape(col_shape), own_mp, 1, keepdims=False)
    matches = col_target[:, :, None] == col_target[:, None, :]
    earlier = lax.broadcasted_iota(jnp.int32, (in_slots, in_slots), 0) < lax.broadcasted_iota(
        jnp.int32, (in_slots, in_slots), 1
    )
    arrival_rank = jnp.sum((matches & earlier[None]).astype(jnp.int32), axis=1)
    sources = lax.broadcasted_iota(jnp.int32, (n_dp, in_slots), 0)
    arrive = sources * capacity + arrival_rank
    own_target = lax.dynamic_index_in_dim(col_target, own_dp, 0, keepdims=False)
    own_rank = lax.dynamic_index_in_dim(arrival_rank, own_dp, 0, keepdims=False)
    send_slot = jnp.where(own_target >= 0, own_target * capacity + own_rank, n_dp * capacity)
    chosen = (
        jnp.full((n_dp * capacity,), in_slots, jnp.int32)
        .at[send_slot]
        .set(jnp.arange(in_slots, dtype=jnp.int32), mode="drop")
    )
    landing = jnp.where(col_target == own_dp, col_slot, OUT_SLOTS).reshape(-1)
    gather_order = (
        jnp.zeros((OUT_SLOTS,), jnp.int32).at[landing].set(arrive.reshape(-1), mode="drop")
    )
    out_fill = jnp.zeros((OUT_SLOTS,), jnp.int32).at[landing].set(col_fill.reshape(-1), mode="drop")
    own_fill = lax.dynamic_index_in_dim(col_fill, own_dp, 0, keepdims=False)
    return (chosen, gather_order, out_fill, own_fill)


def statistics(blocks, fills, proj_weight, proj_bias):
    logits = (
        jnp.einsum("nkd,bd->nbk", blocks, proj_weight, preferred_element_type=jnp.float32)
        + proj_bias[None, :, None]
    )
    scaled = sharpness * logits
    token_mask = (lax.broadcasted_iota(jnp.int32, (1, 1, BLK), 2) < fills[:, None, None]).astype(
        jnp.float32
    )
    probability = jax.nn.sigmoid(scaled)
    entropy = jax.nn.softplus(scaled) - probability * scaled
    bit_sums = jnp.sum(probability * token_mask, axis=(0, 2))
    entropy_sum = jnp.sum(entropy * token_mask)
    variance = probability * (1.0 - probability) * token_mask
    return (bit_sums, entropy_sum, -2.0 * scaled * variance, 2.0 * variance)


def local(latents, proj_weight, proj_bias, fill, target, target_slot):
    n_dp = lax.axis_size("dp")
    n_mp = lax.axis_size("mp")
    own_dp = lax.axis_index("dp")
    own_mp = lax.axis_index("mp")
    feature_width = latents.shape[1]
    in_slots = latents.shape[0] // BLK
    capacity = max(1, 2 * OUT_SLOTS // n_dp)
    chosen, gather_order, out_fill, own_fill = routing(
        fill, target, target_slot, n_dp, n_mp, in_slots, capacity, own_dp, own_mp
    )
    token_count = jnp.sum(fill).astype(jnp.float32)
    loaded = latents.reshape(in_slots, BLK, feature_width)
    bit_sums, entropy_sum, first_term, second_term = statistics(
        loaded, own_fill, proj_weight, proj_bias
    )
    first_rounded = first_term.astype(jnp.bfloat16)
    second_rounded = second_term.astype(jnp.bfloat16)
    first_weight = jnp.einsum(
        "nbk,nkd->bd", first_rounded, loaded, preferred_element_type=jnp.float32
    )
    second_weight = jnp.einsum(
        "nbk,nkd->bd", second_rounded, loaded, preferred_element_type=jnp.float32
    )
    bit_sums, entropy_sum = lax.psum((bit_sums, entropy_sum), ("dp", "mp"))
    marginal = bit_sums / token_count
    codebook = -jnp.sum(marginal * jnp.log(marginal) + (1.0 - marginal) * jnp.log(1.0 - marginal))
    entropy_loss = entropy_sum / token_count - codebook
    log_odds = jnp.log(1.0 - marginal) - jnp.log(marginal)
    cotangent = (first_term - second_term * log_odds[None, :, None]).astype(jnp.bfloat16)
    padded_cot = jnp.concatenate(
        [cotangent, jnp.zeros((1,) + cotangent.shape[1:], cotangent.dtype)]
    )
    outgoing_cot = padded_cot[chosen].reshape(n_dp * capacity * cotangent.shape[1], BLK)
    arrived_cot = lax.all_to_all(outgoing_cot, "dp", split_axis=0, concat_axis=0, tiled=True)
    landed = arrived_cot.reshape(n_dp * capacity, cotangent.shape[1], BLK)[gather_order]
    latent_grad = jnp.einsum(
        "nbk,bd->nkd", landed, proj_weight, preferred_element_type=jnp.float32
    ).astype(jnp.bfloat16)
    first_weight, second_weight = lax.psum((first_weight, second_weight), ("dp", "mp"))
    weight_grad = (first_weight - second_weight * log_odds[:, None]) / jnp.sqrt(token_count)
    return (latent_grad.reshape(-1, feature_width), weight_grad, entropy_loss)


def solution(mesh):
    placed = (P(("dp", "mp"), None), P(), P(), P(), P(), P())
    return jax.shard_map(
        local,
        mesh=mesh,
        in_specs=placed,
        out_specs=(P(("dp", "mp"), None), P(), P()),
        check_vma=False,
    )
```

profile of v0, /device:TPU:0, one launch (start us, length us, event | category | flops | bytes accessed | tf_op | source)
XLA Modules:
  0.0 73.5 jit_solution(14534599684617418197)
XLA Ops:
  0.6 0.0 copy-start
  0.7 0.8 %reshape.158 = s32[8,4,64]{2,1,0:T(4,128)S(1)} reshape(s32[2048]{0:T(1024)} %param.9) | data formatting | bytes 16384 | tf_op jit(solution)/shard_map/reshape | solution.py:15
  1.4 1.3 %reduce_sum.46 = s32[]{:T(128)} reduce(s32[2048]{0:T(1024)} %param.9, s32[]{:T(128)} %constant.78.clone.1), dimensions={0}, to_apply=%region_2.3 | reduce | flops 2047 | bytes 8200 | tf_op jit(solution)/shard_map/reduce_sum | solution.py:70
  2.8 0.1 fusion.19
  2.9 0.0 copy-done
  2.9 0.0 copy-start.3
  2.9 4.2 %fusion.3 = (f32[]{:T(128)}, f32[18]{0:T(128)S(1)}, f32[18,64,128]{2,0,1:T(8,128)S(1)}) fusion(f32[64,128]{1,0:T(8,128)S(1)} %fusion.19, f32[18]{0:T(128)} %param.8, bf16[64,128,256]{2,1,0:T(8,128)(2,1)} %bitcast.89, bf16[18,256]{1,0:T(8,128)(2,1)S(1)} %copy-done), kind=kOutput, calls=%fused_computation.13 | convolution fusion | flops 78004208 | bytes 4826260 | tf_op jit(solution)/shard_map/nkd,bd->nbk/dot_general | solution.py:44
  7.1 0.0 copy-done.3
  7.1 0.8 %convolution_bitcast_fusion.1 = f32[18,256]{1,0:T(8,128)S(1)} fusion(bf16[64,128,256]{2,1,0:T(8,128)(2,1)S(1)} %bitcast.90, f32[18,64,128]{2,0,1:T(8,128)S(1)} %get-tuple-element.15, f32[64,128]{1,0:T(8,128)S(1)} %fusion.19), kind=kOutput, calls=%fused_computation.9 | convolution fusion | flops 76972032 | bytes 4835328 | tf_op jit(solution)/shard_map/nbk,nkd->bd/dot_general | solution.py:77
  7.9 0.0 copy-start.1
  7.9 0.0 copy-start.2
  7.9 0.8 %convolution_bitcast_fusion = f32[18,256]{1,0:T(8,128)S(1)} fusion(bf16[64,128,256]{2,1,0:T(8,128)(2,1)S(1)} %bitcast.91, f32[64,128]{1,0:T(8,128)S(1)} %fusion.19, f32[18,64,128]{2,0,1:T(8,128)S(1)} %get-tuple-element.15), kind=kOutput, calls=%fused_computation.8 | convolution fusion | flops 76824576 | bytes 4835328 | tf_op jit(solution)/shard_map/nbk,nkd->bd/dot_general | solution.py:80
  9.4 0.0 copy-done.1
  9.4 0.1 reshape.159
  9.5 0.0 copy-done.2
  9.5 0.1 reshape.161
  9.6 0.1 convert_reduce_fusion
  9.7 0.8 %scatter_custom_fusion = s32[64]{0:T(128)S(1)} fusion(s32[64]{0:T(128)S(1)} %fusion.27, s32[64]{0:T(128)S(1)} %iota.34, s32[]{:T(128)} %constant.88.clone.1), kind=kCustom, calls=%fused_computation.69 | custom fusion | bytes 260 | tf_op jit(solution)/shard_map/scatter | solution.py:31
  10.6 42.8 %all-reduce.1 = (f32[18]{0:T(128)S(1)}, f32[18,256]{1,0:T(8,128)S(1)}, f32[18,256]{1,0:T(8,128)S(1)}, f32[]{:T(128)}) all-reduce(f32[18]{0:T(128)S(1)} %get-tuple-element.4, f32[18,256]{1,0:T(8,128)S(1)} %convolution_bitcast_fusion.1, f32[18,256]{1,0:T(8,128)S(1)} %convolution_bitcast_fusion, ...), channel_id=1, replica_groups=mesh['dp'=8,'mp'=4] {'dp','mp'}, use_global_device_ids=true, to_apply=%region_1.2 | all-reduce | flops 9235 | bytes 73880 | tf_op jit(solution)/shard_map/psum | solution.py:83
  53.3 0.6 fusion.28
  53.9 0.4 subtract_convert_fusion
  54.4 0.7 gather_fusion
  55.0 0.8 %all_to_all.6 = bf16[8,144,128]{2,1,0:T(8,128)(2,1)} reshape(bf16[64,18,128]{2,1,0:T(8,128)(2,1)S(1)} %gather_fusion) | data formatting | bytes 589824 | tf_op jit(solution)/shard_map/all_to_all | solution.py:93
  55.8 5.3 %all-to-all-start = ((bf16[8,144,128]{2,1,0:T(8,128)(2,1)}), bf16[8,144,128]{2,1,0:T(8,128)(2,1)S(1)}, u32[]{:S(2)}, u32[]{:S(2)}) async-start(bf16[8,144,128]{2,1,0:T(8,128)(2,1)} %all_to_all.6), calls=%async_computation | async-start | bytes 589824 | tf_op jit(solution)/shard_map/all_to_all | solution.py:93
  61.2 0.1 select_n.80
  61.3 0.1 broadcast_add_fusion
  61.3 0.1 reshape.191
  62.7 2.4 %scatter_custom_fusion.1 = s32[32]{0:T(128)S(1)} fusion(s32[512]{0:T(512)S(1)} %bitcast.88, s32[512]{0:T(512)S(1)} %reshape.191, s32[]{:T(128)} %constant.78.clone.1), kind=kCustom, calls=%fused_computation.67 | custom fusion | bytes 132 | tf_op jit(solution)/shard_map/scatter | solution.py:35
  65.2 0.7 subtract_divide_fusion
  65.9 3.7 %all-to-all-done = bf16[8,144,128]{2,1,0:T(8,128)(2,1)S(1)} async-done(((bf16[8,144,128]{2,1,0:T(8,128)(2,1)}), bf16[8,144,128]{2,1,0:T(8,128)(2,1)S(1)}, u32[]{:S(2)}, u32[]{:S(2)}) %all-to-all-start) | async-done | bytes 294944 | tf_op jit(solution)/shard_map/all_to_all | solution.py:93
  69.6 0.1 reshape.160
  69.7 0.6 gather_fusion.1
  70.3 2.1 %convolution_convert_fusion = bf16[32,128,256]{2,1,0:T(8,128)(2,1)} fusion(bf16[32,18,128]{2,1,0:T(8,128)(2,1)S(1)} %gather_fusion.1, bf16[18,256]{1,0:T(8,128)(2,1)S(1)} %copy-done), kind=kOutput, calls=%fused_computation.5 | convolution fusion | flops 38797312 | bytes 2253824 | tf_op jit(solution)/shard_map/nbk,bd->nkd/dot_general | solution.py:95
  (13 shorter events, 0.1 us)
Async XLA Ops:
  0.6 2.2 %copy-start = (bf16[18,256]{1,0:T(8,128)(2,1)S(1)}, bf16[18,256]{1,0:T(8,128)(2,1)}, u32[]{:S(2)}) copy-start(bf16[18,256]{1,0:T(8,128)(2,1)} %param.7) | copy-start | bytes 27652
  2.9 4.2 %copy-start.3 = (bf16[8192,256]{1,0:T(8,128)(2,1)S(1)}, bf16[8192,256]{1,0:T(8,128)(2,1)}, u32[]{:S(2)}) copy-start(bf16[8192,256]{1,0:T(8,128)(2,1)} %param.6) | copy-start | bytes 12582916
  7.9 1.5 %copy-start.1 = (s32[2048]{0:T(1024)S(1)}, s32[2048]{0:T(1024)}, u32[]{:S(2)}) copy-start(s32[2048]{0:T(1024)} %param.10) | copy-start | bytes 24580
  7.9 1.5 %copy-start.2 = (s32[2048]{0:T(1024)S(1)}, s32[2048]{0:T(1024)}, u32[]{:S(2)}) copy-start(s32[2048]{0:T(1024)} %param.11) | copy-start | bytes 24580
  55.8 13.7 %all-to-all-start = ((bf16[8,144,128]{2,1,0:T(8,128)(2,1)}), bf16[8,144,128]{2,1,0:T(8,128)(2,1)S(1)}, u32[]{:S(2)}, u32[]{:S(2)}) async-start(bf16[8,144,128]{2,1,0:T(8,128)(2,1)} %all_to_all.6), calls=%async_computation | async-start | bytes 589824 | tf_op jit(solution)/shard_map/all_to_all | solution.py:93
where the time goes:
time: 74 us; the launch traced here: 73.5 us
  blocking collectives  42.8 us (58%)
  matrix products  7.88 us (11%)
  local copies, waits for them, and re-layouts  6.53 us (9%)
  starting transfers between devices  5.29 us (7%)
  between operations  3.96 us (5%)
  waiting for transfers between devices  3.68 us (5%)
  other arithmetic  3.36 us (5%)
    psum x1, blocking collectives, local(): bit_sums, entropy_sum = lax.psum((bit_sums, entropy_sum), ('dp', 'mp'))  42.8 us
    all_to_all x1, starting transfers between devices, local(): lax.all_to_all(outgoing_cot, 'dp', split_axis=0, concat_axis=0, tiled=True)  5.29 us
    dot_general x1, matrix products, statistics(): jnp.einsum('nkd,bd->nbk', blocks, proj_weight, preferred_element_type=jnp...  4.21 us
    all_to_all x1, waiting for transfers between devices, local(): lax.all_to_all(outgoing_cot, 'dp', split_axis=0, concat_axis=0, tiled=True)  3.68 us
    scatter x1, local copies, waits for them, and re-layouts, routing(): jnp.zeros((OUT_SLOTS,), jnp.int32).at[landing]  2.44 us
    dot_general x1, matrix products, local(): jnp.einsum('nbk,bd->nkd', landed, proj_weight, preferred_element_type=jnp...  2.08 us
  transfers between devices with their start and end apart: 1, of which 1 were waited for; matrix products, arithmetic and copies ran while one was open for 5% of the time, Pallas kernels for 0%

commit v1 on v0

v1 whole, which is shorter than its diff:
```python
import functools

import jax
import jax.numpy as jnp
from jax import lax
from jax.experimental import pallas as pl
from jax.experimental.pallas import tpu as pltpu
from jax.sharding import PartitionSpec as P

BLK = 128
OUT_SLOTS = 32
LANES = 128
F32 = jnp.float32
BF16 = jnp.bfloat16
MESH = pl.DeviceIdType.MESH

sharpness = 2.0


def routing(target, target_slot, n_dp, n_mp, in_slots, capacity, own_dp, own_mp):
    shape = (n_dp, n_mp, in_slots)
    col_target = lax.dynamic_index_in_dim(target.reshape(shape), own_mp, 1, keepdims=False)
    col_slot = lax.dynamic_index_in_dim(target_slot.reshape(shape), own_mp, 1, keepdims=False)
    own_target = lax.dynamic_index_in_dim(col_target, own_dp, 0, keepdims=False)
    slots = jnp.arange(in_slots, dtype=jnp.int32)
    earlier = slots[:, None] < slots[None, :]
    own_rank = jnp.sum(((own_target[:, None] == own_target[None, :]) & earlier).astype(jnp.int32), axis=0)
    position = jnp.where(own_target >= 0, own_target * capacity + own_rank, -1)
    sends = jnp.arange(n_dp * capacity, dtype=jnp.int32)
    chosen = jnp.sum(jnp.where(position[None, :] == sends[:, None], slots[None, :], 0), axis=1)
    mine = col_target == own_dp
    rank = jnp.sum((mine[:, :, None] & earlier[None]).astype(jnp.int32), axis=1)
    arrive = jnp.arange(n_dp, dtype=jnp.int32)[:, None] * capacity + rank
    outs = jnp.arange(OUT_SLOTS, dtype=jnp.int32)[:, None, None]
    order = jnp.sum(jnp.where(mine[None] & (col_slot[None] == outs), arrive[None], 0), axis=(1, 2))
    return chosen, order


def wait_bytes(ref, sem):
    pltpu.make_async_copy(ref, ref, sem).wait()


def to_column(row, rows):
    a = lax.broadcasted_iota(jnp.int32, (rows, LANES), 0)
    b = lax.broadcasted_iota(jnp.int32, (rows, LANES), 1)
    return jnp.sum(jnp.where(a == b, jnp.broadcast_to(row, (rows, LANES)), 0.0), axis=1, keepdims=True)


def to_row(column, rows):
    a = lax.broadcasted_iota(jnp.int32, (rows, LANES), 0)
    b = lax.broadcasted_iota(jnp.int32, (rows, LANES), 1)
    return jnp.sum(jnp.where(a == b, jnp.broadcast_to(column, (rows, LANES)), 0.0), axis=0, keepdims=True)


def exchange_kernel(
    n_dp, n_mp, bits, capacity, chunk_slots,
    fill_ref, chosen_ref, count_ref, x_hbm, w_ref, bias_ref,
    land_ref, wg_ref, loss_ref,
    xbuf, first_ref, second_ref, rounded_ref, stat_own, stat_all, send_buf, wg_own, wg_parts, wg_row, wg_all,
    x_sem, stat_send, stat_recv, cot_send, cot_recv, cot_local, part_send, part_recv, row_send, row_recv,
):
    n_dev = n_dp * n_mp
    rows = w_ref.shape[0]
    width = w_ref.shape[1]
    chunk = chunk_slots * BLK
    chunks = xbuf.shape[0] // chunk
    own_dp = lax.axis_index("dp")
    own_mp = lax.axis_index("mp")
    own = own_dp * n_mp + own_mp

    def device(i):
        return {"dp": lax.div(i, n_mp), "mp": lax.rem(i, n_mp)}

    def x_copy(c):
        part = pl.ds(c * chunk, chunk)
        return pltpu.make_async_copy(x_hbm.at[part], xbuf.at[part], x_sem.at[c])

    for c in range(chunks):
        x_copy(c).start()

    barrier = pltpu.get_barrier_semaphore()

    @pl.loop(1, n_dev)
    def _(off):
        pl.semaphore_signal(barrier, inc=1, device_id=device(lax.rem(own + off, n_dev)), device_id_type=MESH)

    bias = bias_ref[...]
    w = w_ref[...]
    live_row = (lax.broadcasted_iota(jnp.int32, (rows, 1), 0) < bits).astype(F32)
    lane = lax.broadcasted_iota(jnp.int32, (1, BLK), 1)

    def statistics(c, carry):
        bit_acc, ent_acc = carry
        x_copy(c).wait()
        x = xbuf[pl.ds(pl.multiple_of(c * chunk, chunk), chunk), :]
        logits = lax.dot_general(w, x, (((1,), (1,)), ((), ())), preferred_element_type=F32) + bias
        scaled = sharpness * logits
        mask = jnp.concatenate(
            [(lane < fill_ref[c * chunk_slots + i]).astype(F32) for i in range(chunk_slots)], axis=1
        )
        size = jnp.abs(scaled)
        e = jnp.exp(-size)
        r = 1.0 / (1.0 + e)
        er = e * r
        prob = jnp.where(scaled >= 0, r, er) * mask
        ent = (jnp.log1p(e) + size * er) * mask
        second = 2.0 * (er * r * mask)
        first = -(scaled * second)
        rounded_ref[c] = jnp.concatenate([first, second], axis=0).astype(BF16)
        for i in range(chunk_slots):
            cols = slice(i * BLK, (i + 1) * BLK)
            first_ref[c * chunk_slots + i] = first[:, cols]
            second_ref[c * chunk_slots + i] = second[:, cols]
            bit_acc = bit_acc + prob[:, cols]
            ent_acc = ent_acc + ent[:, cols]
        return bit_acc, ent_acc

    zero = jnp.zeros((rows, BLK), F32)
    bit_acc, ent_acc = lax.fori_loop(0, chunks, statistics, (zero, zero))
    bit_row = to_row(jnp.sum(bit_acc, axis=1, keepdims=True) * live_row, rows)
    ent_sum = jnp.sum(jnp.sum(ent_acc * live_row, axis=1, keepdims=True), axis=0, keepdims=True)
    lanes = lax.broadcasted_iota(jnp.int32, (1, LANES), 1)
    stat = jnp.where(lanes == LANES - 1, jnp.broadcast_to(ent_sum, (1, LANES)), bit_row)
    stat_own[...] = stat
    stat_all[own] = stat

    pl.semaphore_wait(barrier, n_dev - 1)

    @pl.loop(1, n_dev)
    def _(off):
        pltpu.make_async_remote_copy(
            src_ref=stat_own, dst_ref=stat_all.at[own], send_sem=stat_send, recv_sem=stat_recv,
            device_id=device(lax.rem(own + off, n_dev)), device_id_type=MESH,
        ).start()

    def products(c, acc):
        x = xbuf[pl.ds(pl.multiple_of(c * chunk, chunk), chunk), :]
        return acc + jnp.dot(rounded_ref[c], x, preferred_element_type=F32)

    both = lax.fori_loop(0, chunks, products, jnp.zeros((2 * rows, width), F32))

    wait_bytes(stat_all.at[pl.ds(0, n_dev - 1)], stat_recv)
    total = jnp.sum(stat_all[...], axis=0)
    count = count_ref[0]
    column = to_column(total, rows)
    marginal_c = column / count
    log_odds = jnp.log(1.0 - marginal_c) - jnp.log(marginal_c)
    log_odds = jnp.where(live_row > 0, log_odds, 0.0)

    part = both[:rows] - both[rows:] * log_odds
    for b in range(bits):
        wg_own[b] = part[b:b + 1]

    wg_parts[own] = wg_own[jnp.minimum(own, bits - 1)]

    @pl.loop(0, bits)
    def _(b):
        @pl.when(b != own)
        def _():
            pltpu.make_async_remote_copy(
                src_ref=wg_own.at[b], dst_ref=wg_parts.at[own], send_sem=part_send, recv_sem=part_recv,
                device_id=device(b), device_id_type=MESH,
            ).start()

    @pl.loop(1, n_dp + 1)
    def _(off):
        peer = lax.rem(own_dp + off, n_dp)
        blocks = []
        for k in range(capacity):
            slot = chosen_ref[peer * capacity + k]
            blocks.append((first_ref[slot] - second_ref[slot] * log_odds)[:bits])
        send_buf[peer] = jnp.concatenate(blocks, axis=0).astype(BF16)

        @pl.when(off < n_dp)
        def _():
            pltpu.make_async_remote_copy(
                src_ref=send_buf.at[peer], dst_ref=land_ref.at[own_dp], send_sem=cot_send, recv_sem=cot_recv,
                device_id={"dp": peer, "mp": own_mp}, device_id_type=MESH,
            ).start()

    keep = pltpu.make_async_copy(send_buf.at[own_dp], land_ref.at[own_dp], cot_local)
    keep.start()

    marginal = total / count
    inside = lanes < bits
    safe = jnp.where(inside, marginal, 0.5)
    plain = safe * jnp.log(safe) + (1.0 - safe) * jnp.log(1.0 - safe)
    neg_codebook = jnp.sum(jnp.where(inside, plain, 0.0), axis=1, keepdims=True)
    ent_all = jnp.sum(jnp.where(lanes == LANES - 1, total, 0.0), axis=1, keepdims=True)
    loss_ref[...] = jnp.broadcast_to(ent_all / count + neg_codebook, (1, LANES))

    @pl.when(own < bits)
    def _():
        wait_bytes(wg_parts.at[pl.ds(0, n_dev - 1)], part_recv)
        row = jnp.sum(wg_parts[...], axis=0) / jnp.sqrt(jnp.full((1, width), count, F32))
        wg_row[...] = row
        wg_all[own] = row

        @pl.loop(1, n_dev)
        def _(off):
            pltpu.make_async_remote_copy(
                src_ref=wg_row, dst_ref=wg_all.at[own], send_sem=row_send, recv_sem=row_recv,
                device_id=device(lax.rem(own + off, n_dev)), device_id_type=MESH,
            ).start()

        wait_bytes(wg_all.at[pl.ds(0, bits - 1)], row_recv)
        wait_bytes(wg_own.at[pl.ds(0, bits - 1)], part_send)
        wait_bytes(wg_parts.at[pl.ds(0, n_dev - 1)], row_send)

    @pl.when(own >= bits)
    def _():
        wait_bytes(wg_all.at[pl.ds(0, bits)], row_recv)
        wait_bytes(wg_own.at[pl.ds(0, bits)], part_send)

    wg_ref[...] = wg_all[...]
    wait_bytes(stat_all.at[pl.ds(0, n_dev - 1)], stat_send)
    keep.wait()
    wait_bytes(send_buf.at[pl.ds(0, n_dp - 1)], cot_send)
    wait_bytes(land_ref.at[pl.ds(0, n_dp - 1)], cot_recv)


def finish_kernel(n_dp, bits, capacity, step_blocks, order_ref, land_ref, w_ref, wg_ref, out_ref, wg_out, blocks):
    @pl.when(pl.program_id(0) == 0)
    def _():
        for src in range(n_dp):
            rows = land_ref[src].astype(F32)
            for k in range(capacity):
                blocks[src * capacity + k] = rows[k * bits:(k + 1) * bits]
        for b in range(bits):
            wg_out[b:b + 1, :] = wg_ref[b]

    w = w_ref[...]
    for i in range(step_blocks):
        cot = blocks[order_ref[pl.program_id(0) * step_blocks + i]].astype(BF16)
        out_ref[i * BLK:(i + 1) * BLK, :] = lax.dot_general(
            cot, w, (((0,), (0,)), ((), ())), preferred_element_type=F32
        ).astype(BF16)


def local(latents, proj_weight, proj_bias, fill, target, target_slot):
    n_dp = lax.axis_size("dp")
    n_mp = lax.axis_size("mp")
    n_dev = n_dp * n_mp
    own_dp = lax.axis_index("dp")
    own_mp = lax.axis_index("mp")
    width = latents.shape[1]
    bits = proj_weight.shape[0]
    in_slots = latents.shape[0] // BLK
    capacity = max(1, 2 * OUT_SLOTS // n_dp)
    rows = -(-bits // 8) * 8
    chunk_slots = 8
    chunks = in_slots // chunk_slots
    chosen, order = routing(target, target_slot, n_dp, n_mp, in_slots, capacity, own_dp, own_mp)
    own_fill = lax.dynamic_slice(fill, ((own_dp * n_mp + own_mp) * in_slots,), (in_slots,))
    count = jnp.sum(fill).astype(F32).reshape(1)
    w_pad = jnp.pad(proj_weight, ((0, rows - bits), (0, 0)))
    bias_pad = jnp.pad(proj_bias, (0, rows - bits)).reshape(rows, 1)
    smem = pl.BlockSpec(memory_space=pltpu.SMEM)
    vmem = pl.BlockSpec(memory_space=pltpu.VMEM)
    hbm = pl.BlockSpec(memory_space=pl.ANY)
    dma = pltpu.SemaphoreType.DMA
    land, wg, loss = pl.pallas_call(
        functools.partial(exchange_kernel, n_dp, n_mp, bits, capacity, chunk_slots),
        out_shape=(
            jax.ShapeDtypeStruct((n_dp, capacity * bits, BLK), BF16),
            jax.ShapeDtypeStruct((bits, 1, width), F32),
            jax.ShapeDtypeStruct((1, LANES), F32),
        ),
        in_specs=[smem, smem, smem, hbm, vmem, vmem],
        out_specs=(hbm, vmem, vmem),
        scratch_shapes=[
            pltpu.VMEM(latents.shape, BF16),
            pltpu.VMEM((in_slots, rows, BLK), F32),
            pltpu.VMEM((in_slots, rows, BLK), F32),
            pltpu.VMEM((chunks, 2 * rows, chunk_slots * BLK), BF16),
            pltpu.VMEM((1, LANES), F32),
            pltpu.VMEM((n_dev, 1, LANES), F32),
            pltpu.VMEM((n_dp, capacity * bits, BLK), BF16),
            pltpu.VMEM((bits, 1, width), F32),
            pltpu.VMEM((n_dev, 1, width), F32),
            pltpu.VMEM((1, width), F32),
            pltpu.VMEM((bits, 1, width), F32),
            dma((chunks,)),
        ] + [dma(())] * 9,
        compiler_params=pltpu.CompilerParams(
            collective_id=0, has_side_effects=True, vmem_limit_bytes=32 * 1024 * 1024
        ),
        name="exchange",
    )(own_fill, chosen, count, latents, w_pad, bias_pad)
    step_blocks = 8
    grad, wg = pl.pallas_call(
        functools.partial(finish_kernel, n_dp, bits, capacity, step_blocks),
        out_shape=(
            jax.ShapeDtypeStruct((OUT_SLOTS * BLK, width), BF16),
            jax.ShapeDtypeStruct((bits, width), F32),
        ),
        grid_spec=pltpu.PrefetchScalarGridSpec(
            num_scalar_prefetch=1,
            grid=(OUT_SLOTS // step_blocks,),
            in_specs=[vmem, vmem, vmem],
            out_specs=(
                pl.BlockSpec((step_blocks * BLK, width), lambda g, order: (g, 0)),
                pl.BlockSpec((bits, width), lambda g, order: (0, 0)),
            ),
            scratch_shapes=[pltpu.VMEM((n_dp * capacity, bits, BLK), F32)],
        ),
        name="finish",
    )(order, land, proj_weight, wg)
    return grad, wg, loss[0, 0]


def solution(mesh):
    placed = (P(("dp", "mp"), None), P(), P(), P(), P(), P())
    return jax.shard_map(
        local,
        mesh=mesh,
        in_specs=placed,
        out_specs=(P(("dp", "mp"), None), P(), P()),
        check_vma=False,
    )
```

time: 74 us -> 39.4 us (0.53)
  blocking collectives: 42.8 us -> 0 us
  Pallas kernels: 0 us -> 26.2 us
  matrix products: 7.88 us -> 0 us
  starting transfers between devices: 5.29 us -> 0 us
  waiting for transfers between devices: 3.68 us -> 0 us
  between operations: 3.96 us -> 2.52 us
  local copies, waits for them, and re-layouts: 6.53 us -> 7.29 us
    psum x1 -> x0, blocking collectives: 42.8 us -> none  [local(): bit_sums, entropy_sum = lax.psum((bit_sums, entropy_sum), ('dp', 'mp'))]
    pallas_call x0 -> x2, Pallas kernels: none -> 26.2 us  [the longest x1 21.9 us: local(): pl.pallas_call(functools.partial(exchange_kernel, n_dp, n_mp, bits, capac...]
    dot_general x4 -> x0, matrix products: 7.88 us -> none  [the longest x1 4.21 us: statistics(): jnp.einsum('nkd,bd->nbk', blocks, proj_weight, preferred_element_type=jnp...]
    all_to_all x1 -> x0, starting transfers between devices: 5.29 us -> none  [local(): lax.all_to_all(outgoing_cot, 'dp', split_axis=0, concat_axis=0, tiled=True)]
    all_to_all x1 -> x0, waiting for transfers between devices: 3.68 us -> none  [local(): lax.all_to_all(outgoing_cot, 'dp', split_axis=0, concat_axis=0, tiled=True)]
    unnamed x8 -> x7, local copies, waits for them, and re-layouts: 0.03 us -> 3.49 us
    scatter x2 -> x0, local copies, waits for them, and re-layouts: 3.21 us -> none  [the longest x1 2.44 us: routing(): jnp.zeros((OUT_SLOTS,), jnp.int32).at[landing]]
    reshape x4, local copies, waits for them, and re-layouts: 1.02 us -> 2.3 us  [the longest x1 0.78 us: routing(): target_slot.reshape(shape)]
  transfers between devices with their start and end apart: 1 -> 0, of which waited for: 1 -> 0; matrix products, arithmetic and copies ran while one was open for 5% -> 0% of each run, Pallas kernels for 0% -> 0%
where the time goes in v1:
time: 39.4 us; the launch traced here: 39 us
  Pallas kernels  26.2 us (66%)
  local copies, waits for them, and re-layouts  7.29 us (19%)
  other arithmetic  2.97 us (8%)
  between operations  2.52 us (6%)
    pallas_call x1, Pallas kernels, local(): pl.pallas_call(functools.partial(exchange_kernel, n_dp, n_mp, bits, capac...  21.9 us
    pallas_call x1, Pallas kernels, local(): pl.pallas_call(functools.partial(finish_kernel, n_dp, bits, capacity, ste...  4.32 us
    unnamed x7, local copies, waits for them, and re-layouts  3.49 us
    reduce_sum x1, other arithmetic, local(): count = jnp.sum(fill).astype(F32).reshape(1)  1.34 us
    reduce_sum x1, other arithmetic, routing(): jnp.sum(jnp.where(mine[None] & (col_slot[None] == outs), arrive[None], 0)...  1.18 us

profile of v1, /device:TPU:0, one launch (start us, length us, event | category | flops | bytes accessed | tf_op | source)
XLA Modules:
  0.0 39.0 jit_solution(12237205674125126176)
XLA Ops:
  0.6 1.3 %reduce_sum.49 = s32[]{:T(128)} reduce(s32[2048]{0:T(1024)} %param.9, s32[]{:T(128)} %constant.42.clone.1), dimensions={0}, to_apply=%region_4.5 | reduce | flops 2047 | bytes 8200 | tf_op jit(solution)/shard_map/reduce_sum | solution.py:255
  2.6 0.8 %dynamic_slice.16.fill_ref = s32[64]{0:T(128)S(1)} dynamic-slice(s32[2048]{0:T(1024)} %param.9, s32[]{:T(128)S(6)} %select_n.34), dynamic_slice_sizes={64} | dynamic-slice | bytes 516 | tf_op jit(solution)/shard_map/dynamic_slice | solution.py:254
  3.4 0.7 %pad_bitcast_fusion = f32[24,1]{0,1:T(1,128)S(1)} fusion(f32[18]{0:T(128)} %param.8), kind=kLoop, calls=%fused_computation.15 | loop fusion | bytes 168 | tf_op jit(solution)/shard_map/reshape | solution.py:257
  4.1 0.1 copy.12.bias_ref
  4.2 0.7 %pad.8.w_ref = bf16[24,256]{1,0:T(8,128)(2,1)S(1)} pad(bf16[18,256]{1,0:T(8,128)(2,1)} %w_ref.1, bf16[]{:T(256)} %constant.53.clone.1), padding=0_6x0_0 | pad | bytes 21506 | tf_op jit(solution)/shard_map/jit(_pad)/pad | solution.py:256
  4.9 0.8 %reshape.82 = s32[8,4,64]{2,1,0:T(4,128)S(1)} reshape(s32[2048]{0:T(1024)} %param.10) | data formatting | bytes 16384 | tf_op jit(solution)/shard_map/reshape | solution.py:22
  5.7 0.1 convert_reduce_fusion.1
  5.8 0.1 convert_reduce_fusion
  6.0 0.1 broadcast_add_fusion
  6.0 0.1 select_reduce_fusion.1.chosen_ref
  6.1 0.8 %reshape.83 = s32[8,4,64]{2,1,0:T(4,128)S(1)} reshape(s32[2048]{0:T(1024)} %param.11) | data formatting | bytes 16384 | tf_op jit(solution)/shard_map/reshape | solution.py:23
  6.9 1.2 %select_reduce_fusion.order_ref = s32[32]{0:T(128)} fusion(s32[8,64]{1,0:T(8,128)S(1)} %broadcast_add_fusion, s32[8,64]{1,0:T(8,128)S(1)} %bitcast.14, pred[8,64]{1,0:T(8,128)(4,1)S(1)} %bitcast.16), kind=kLoop, calls=%fused_computation.1 | loop fusion | flops 65504 | bytes 4736 | tf_op jit(solution)/shard_map/reduce_sum | solution.py:35
  8.1 0.0 copy-start
  8.1 2.2 %copy-done = bf16[8192,256]{1,0:T(8,128)(2,1)S(1)} copy-done((bf16[8192,256]{1,0:T(8,128)(2,1)S(1)}, bf16[8192,256]{1,0:T(8,128)(2,1)}, u32[]{:S(2)}) %copy-start) | copy-done | bytes 4194328
  10.3 21.9 %exchange.1 = (bf16[8,144,128]{2,1,0:T(8,128)(2,1)S(1)}, f32[18,1,256]{2,1,0:T(1,128)S(1)}, f32[1,128]{1,0:T(1,128)S(1)}) custom-call(s32[64]{0:T(128)S(1)} %dynamic_slice.16.fill_ref, s32[64]{0:T(128)S(1)} %select_reduce_fusion.1.chosen_ref, f32[1]{0:T(128)} %bitcast.2.count_ref, bf16[8192,256]{1,0:T(8,128)(2,1)S(1)} %copy-done, ...), custom_call_target="tpu_custom_call" | custom-call | tf_op jit(solution)/shard_map/exchange/pallas_call | solution.py:262
  32.2 0.0 copy-start.1
  32.2 0.7 %copy-done.1 = bf16[8,144,128]{2,1,0:T(8,128)(2,1)} copy-done((bf16[8,144,128]{2,1,0:T(8,128)(2,1)}, bf16[8,144,128]{2,1,0:T(8,128)(2,1)S(1)}, u32[]{:S(2)}) %copy-start.1) | copy-done | bytes 294936
  32.9 0.0 copy-start.2
  32.9 0.6 %copy-done.2 = f32[18,1,256]{2,1,0:T(1,128)} copy-done((f32[18,1,256]{2,1,0:T(1,128)}, f32[18,1,256]{2,1,0:T(1,128)S(1)}, u32[]{:S(2)}) %copy-start.2) | copy-done | bytes 18456
  33.5 4.3 %finish.1 = (bf16[4096,256]{1,0:T(8,128)(2,1)}, f32[18,256]{1,0:T(8,128)}) custom-call(s32[32]{0:T(128)} %select_reduce_fusion.order_ref, bf16[8,144,128]{2,1,0:T(8,128)(2,1)} %copy-done.1, bf16[18,256]{1,0:T(8,128)(2,1)} %w_ref.1, f32[18,1,256]{2,1,0:T(1,128)} %copy-done.2), custom_call_target="tpu_custom_call" | custom-call | tf_op jit(solution)/shard_map/finish/pallas_call | solution.py:291
  (7 shorter events, 0.1 us)
Async XLA Ops:
  8.1 2.2 %copy-start = (bf16[8192,256]{1,0:T(8,128)(2,1)S(1)}, bf16[8192,256]{1,0:T(8,128)(2,1)}, u32[]{:S(2)}) copy-start(bf16[8192,256]{1,0:T(8,128)(2,1)} %x_hbm.1) | copy-start | bytes 12582916
  32.2 0.7 %copy-start.1 = (bf16[8,144,128]{2,1,0:T(8,128)(2,1)}, bf16[8,144,128]{2,1,0:T(8,128)(2,1)S(1)}, u32[]{:S(2)}) copy-start(bf16[8,144,128]{2,1,0:T(8,128)(2,1)S(1)} %get-tuple-element.8.land_ref) | copy-start | bytes 884740
  32.9 0.6 %copy-start.2 = (f32[18,1,256]{2,1,0:T(1,128)}, f32[18,1,256]{2,1,0:T(1,128)S(1)}, u32[]{:S(2)}) copy-start(f32[18,1,256]{2,1,0:T(1,128)S(1)} %get-tuple-element.9.wg_ref) | copy-start | bytes 55300

commit v2 on v1

v2 whole, which is shorter than its diff:
```python
import functools

import jax
import jax.numpy as jnp
from jax import lax
from jax.experimental import pallas as pl
from jax.experimental.pallas import tpu as pltpu
from jax.sharding import PartitionSpec as P

BLK = 128
OUT_SLOTS = 32
LANES = 128
F32 = jnp.float32
BF16 = jnp.bfloat16
MESH = pl.DeviceIdType.MESH

sharpness = 2.0


def wait_bytes(ref, sem):
    pltpu.make_async_copy(ref, ref, sem).wait()


def to_column(row, rows):
    shape = (rows, row.shape[1])
    diagonal = lax.broadcasted_iota(jnp.int32, shape, 0) == lax.broadcasted_iota(jnp.int32, shape, 1)
    return jnp.sum(jnp.where(diagonal, jnp.broadcast_to(row, shape), 0.0), axis=1, keepdims=True)


def to_row(column):
    shape = (column.shape[0], LANES)
    diagonal = lax.broadcasted_iota(jnp.int32, shape, 0) == lax.broadcasted_iota(jnp.int32, shape, 1)
    return jnp.sum(jnp.where(diagonal, jnp.broadcast_to(column, shape), 0.0), axis=0, keepdims=True)


def slot_row(ref, index, in_slots):
    per = LANES // in_slots
    line = ref[pl.ds(lax.div(index, per), 1), :].astype(F32)
    which = lax.rem(index, per)
    row = line[:, :in_slots]
    for i in range(1, per):
        row = jnp.where(which == i, line[:, i * in_slots:(i + 1) * in_slots], row)
    return row


def exchange_kernel(
    n_dp, n_mp, bits, capacity, chunk_slots,
    fill_hbm, target_hbm, slot_hbm, x_hbm, w_ref, bias_ref,
    cot_ref, wg_ref, loss_ref,
    xbuf, fill_ref, target_ref, slot_ref, mask_ref, first_ref, second_ref, rounded_ref, stat_own, stat_all,
    send_buf, land, landed, mine_ref, index_vec, chosen_ref, order_ref, wg_own, wg_parts, wg_row, wg_all,
    x_sem, small_sem, index_sem, stat_send, stat_recv, cot_send, cot_recv, part_send, part_recv, row_send, row_recv,
):
    n_dev = n_dp * n_mp
    rows = first_ref.shape[1]
    in_slots = first_ref.shape[0]
    width = w_ref.shape[1]
    out_slots = cot_ref.shape[1] // BLK
    chunk = chunk_slots * BLK
    chunks = xbuf.shape[0] // chunk
    own_dp = lax.axis_index("dp")
    own_mp = lax.axis_index("mp")
    own = own_dp * n_mp + own_mp

    def device(i):
        return {"dp": lax.div(i, n_mp), "mp": lax.rem(i, n_mp)}

    def x_copy(c):
        part = pl.ds(c * chunk, chunk)
        return pltpu.make_async_copy(x_hbm.at[part], xbuf.at[part], x_sem.at[c])

    small = [
        pltpu.make_async_copy(src, dst, small_sem.at[i])
        for i, (src, dst) in enumerate(((fill_hbm, fill_ref), (target_hbm, target_ref), (slot_hbm, slot_ref)))
    ]
    for copy in small:
        copy.start()
    for c in range(chunks):
        x_copy(c).start()

    barrier = pltpu.get_barrier_semaphore()

    @pl.loop(1, n_dev)
    def _(off):
        pl.semaphore_signal(barrier, inc=1, device_id=device(lax.rem(own + off, n_dev)), device_id_type=MESH)

    bias = to_column(bias_ref[...], rows)
    w = w_ref[...]
    w = jnp.concatenate([w.astype(F32), jnp.zeros((rows - bits, width), F32)], axis=0).astype(BF16)
    for copy in small:
        copy.wait()
    fill_col = to_column(slot_row(fill_ref, own, in_slots), in_slots)
    token = lax.broadcasted_iota(jnp.int32, (in_slots, BLK), 1).astype(F32)
    mask_ref[...] = (token < fill_col).astype(F32)
    fills = fill_ref[...].astype(F32)
    count = jnp.sum(jnp.sum(fills, axis=0, keepdims=True), axis=1, keepdims=True)
    live_row = (lax.broadcasted_iota(jnp.int32, (rows, 1), 0) < bits).astype(F32)

    def statistics(c, carry):
        bit_acc, ent_acc = carry
        x_copy(c).wait()
        x = xbuf[pl.ds(pl.multiple_of(c * chunk, chunk), chunk), :]
        logits = lax.dot_general(w, x, (((1,), (1,)), ((), ())), preferred_element_type=F32) + bias
        scaled = sharpness * logits
        mask = jnp.concatenate(
            [mask_ref[pl.ds(c * chunk_slots + i, 1), :] for i in range(chunk_slots)], axis=1
        )
        size = jnp.abs(scaled)
        e = jnp.exp(-size)
        r = 1.0 / (1.0 + e)
        er = e * r
        prob = jnp.where(scaled >= 0, r, er) * mask
        ent = (jnp.log1p(e) + size * er) * mask
        second = 2.0 * (er * r * mask)
        first = -(scaled * second)
        rounded_ref[c] = jnp.concatenate([first, second], axis=0).astype(BF16)
        for i in range(chunk_slots):
            cols = slice(i * BLK, (i + 1) * BLK)
            first_ref[c * chunk_slots + i] = first[:, cols]
            second_ref[c * chunk_slots + i] = second[:, cols]
            bit_acc = bit_acc + prob[:, cols]
            ent_acc = ent_acc + ent[:, cols]
        return bit_acc, ent_acc

    zero = jnp.zeros((rows, BLK), F32)
    bit_acc, ent_acc = lax.fori_loop(0, chunks, statistics, (zero, zero))
    bit_row = to_row(jnp.sum(bit_acc, axis=1, keepdims=True) * live_row)
    ent_sum = jnp.sum(jnp.sum(ent_acc * live_row, axis=1, keepdims=True), axis=0, keepdims=True)
    lanes = lax.broadcasted_iota(jnp.int32, (1, LANES), 1)
    stat = jnp.where(lanes == LANES - 1, jnp.broadcast_to(ent_sum, (1, LANES)), bit_row)
    stat_own[...] = stat
    stat_all[own] = stat

    pl.semaphore_wait(barrier, n_dev - 1)

    @pl.loop(1, n_dev)
    def _(off):
        pltpu.make_async_remote_copy(
            src_ref=stat_own, dst_ref=stat_all.at[own], send_sem=stat_send, recv_sem=stat_recv,
            device_id=device(lax.rem(own + off, n_dev)), device_id_type=MESH,
        ).start()

    target_row = slot_row(target_ref, own, in_slots)
    target_col = to_column(target_row, in_slots)
    before = lax.broadcasted_iota(jnp.int32, (in_slots, in_slots), 1) < lax.broadcasted_iota(
        jnp.int32, (in_slots, in_slots), 0
    )
    rank = jnp.sum(jnp.where((target_col == target_row) & before, 1.0, 0.0), axis=1, keepdims=True)
    position = jnp.where(target_col >= 0.0, target_col * float(capacity) + rank, -1.0)
    send_lane = lax.broadcasted_iota(jnp.int32, (in_slots, LANES), 1).astype(F32)
    send_slot = lax.broadcasted_iota(jnp.int32, (in_slots, LANES), 0).astype(F32)
    chosen = jnp.sum(jnp.where(position == send_lane, send_slot, 0.0), axis=0, keepdims=True)
    index_vec[0] = chosen.astype(jnp.int32)
    choose = pltpu.make_async_copy(index_vec.at[0], chosen_ref, index_sem.at[0])
    choose.start()

    def products(c, acc):
        x = xbuf[pl.ds(pl.multiple_of(c * chunk, chunk), chunk), :]
        return acc + jnp.dot(rounded_ref[c], x, preferred_element_type=F32)

    both = lax.fori_loop(0, chunks, products, jnp.zeros((2 * rows, width), F32))

    wait_bytes(stat_all.at[pl.ds(0, n_dev - 1)], stat_recv)
    total = jnp.sum(stat_all[...], axis=0)
    column = to_column(total, rows)
    marginal_c = column / count
    log_odds = jnp.log(1.0 - marginal_c) - jnp.log(marginal_c)
    log_odds = jnp.where(live_row > 0, log_odds, 0.0)

    choose.wait()
    part = both[:rows] - both[rows:] * log_odds
    for b in range(bits):
        wg_own[b] = part[b:b + 1]

    wg_parts[own] = wg_own[jnp.minimum(own, bits - 1)]

    @pl.loop(0, bits)
    def _(b):
        @pl.when(b != own)
        def _():
            pltpu.make_async_remote_copy(
                src_ref=wg_own.at[b], dst_ref=wg_parts.at[own], send_sem=part_send, recv_sem=part_recv,
                device_id=device(b), device_id_type=MESH,
            ).start()

    @pl.loop(1, n_dp + 1)
    def _(off):
        peer = lax.rem(own_dp + off, n_dp)
        blocks = []
        for k in range(capacity):
            slot = jnp.clip(chosen_ref[0, peer * capacity + k], 0, in_slots - 1)
            blocks.append((first_ref[slot] - second_ref[slot] * log_odds)[:bits])
        packed = jnp.concatenate(blocks, axis=0).astype(BF16)

        @pl.when(off == n_dp)
        def _():
            land[own_dp] = packed

        @pl.when(off < n_dp)
        def _():
            send_buf[peer] = packed
            pltpu.make_async_remote_copy(
                src_ref=send_buf.at[peer], dst_ref=land.at[own_dp], send_sem=cot_send, recv_sem=cot_recv.at[own_dp],
                device_id={"dp": peer, "mp": own_mp}, device_id_type=MESH,
            ).start()

    for d in range(n_dp):
        mine_ref[d:d + 1, :] = jnp.where(slot_row(target_ref, d * n_mp + own_mp, in_slots) == own_dp.astype(F32), 1.0, 0.0)
    mine = mine_ref[...]
    later = lax.broadcasted_iota(jnp.int32, (in_slots, in_slots), 0) < lax.broadcasted_iota(
        jnp.int32, (in_slots, in_slots), 1
    )
    ranks = jnp.dot(mine.astype(BF16), later.astype(F32).astype(BF16), preferred_element_type=F32)
    out_index = lax.broadcasted_iota(jnp.int32, (out_slots, in_slots), 0).astype(F32)
    gathered = jnp.zeros((out_slots, in_slots), F32)
    for d in range(n_dp):
        slots = slot_row(slot_ref, d * n_mp + own_mp, in_slots)
        arrive = float(d * capacity) + ranks[d:d + 1]
        gathered = gathered + jnp.where((out_index == slots) & (mine[d:d + 1] > 0.0), arrive, 0.0)
    order = to_row(jnp.sum(gathered, axis=1, keepdims=True))
    index_vec[1] = order.astype(jnp.int32)
    ordering = pltpu.make_async_copy(index_vec.at[1], order_ref, index_sem.at[1])
    ordering.start()

    marginal = total / count
    inside = lanes < bits
    safe = jnp.where(inside, marginal, 0.5)
    plain = safe * jnp.log(safe) + (1.0 - safe) * jnp.log(1.0 - safe)
    neg_codebook = jnp.sum(jnp.where(inside, plain, 0.0), axis=1, keepdims=True)
    ent_all = jnp.sum(jnp.where(lanes == LANES - 1, total, 0.0), axis=1, keepdims=True)
    loss_ref[...] = jnp.broadcast_to(ent_all / count + neg_codebook, (1, LANES))

    @pl.when(own < bits)
    def _():
        wait_bytes(wg_parts.at[pl.ds(0, n_dev - 1)], part_recv)
        row = jnp.sum(wg_parts[...], axis=0) / jnp.sqrt(count)
        wg_row[...] = row
        wg_all[own] = row

        @pl.loop(1, n_dev)
        def _(off):
            pltpu.make_async_remote_copy(
                src_ref=wg_row, dst_ref=wg_all.at[own], send_sem=row_send, recv_sem=row_recv,
                device_id=device(lax.rem(own + off, n_dev)), device_id_type=MESH,
            ).start()

        wait_bytes(wg_all.at[pl.ds(0, bits - 1)], row_recv)
        wait_bytes(wg_own.at[pl.ds(0, bits - 1)], part_send)
        wait_bytes(wg_parts.at[pl.ds(0, n_dev - 1)], row_send)

    @pl.when(own >= bits)
    def _():
        wait_bytes(wg_all.at[pl.ds(0, bits)], row_recv)
        wait_bytes(wg_own.at[pl.ds(0, bits)], part_send)

    wg_ref[...] = wg_all[...]
    wait_bytes(stat_all.at[pl.ds(0, n_dev - 1)], stat_send)
    ordering.wait()

    @pl.loop(0, n_dp)
    def _(off):
        src = lax.rem(own_dp + n_dp - off, n_dp)

        @pl.when(off > 0)
        def _():
            wait_bytes(land.at[src], cot_recv.at[src])

        arrived = land[src].astype(F32)
        for k in range(capacity):
            landed[src * capacity + k] = arrived[k * bits:(k + 1) * bits]

    for k in range(out_slots):
        cot_ref[:, k * BLK:(k + 1) * BLK] = landed[jnp.clip(order_ref[0, k], 0, n_dp * capacity - 1)].astype(BF16)
    wait_bytes(send_buf.at[pl.ds(0, n_dp - 1)], cot_send)


def finish_kernel(cot_ref, w_ref, wg_ref, out_ref, wg_out):
    @pl.when(pl.program_id(0) == 0)
    def _():
        for b in range(wg_ref.shape[0]):
            wg_out[b:b + 1, :] = wg_ref[b]

    out_ref[...] = lax.dot_general(
        cot_ref[...], w_ref[...], (((0,), (0,)), ((), ())), preferred_element_type=F32
    ).astype(BF16)


def local(latents, proj_weight, proj_bias, fill, target, target_slot):
    n_dp = lax.axis_size("dp")
    n_mp = lax.axis_size("mp")
    n_dev = n_dp * n_mp
    width = latents.shape[1]
    bits = proj_weight.shape[0]
    in_slots = latents.shape[0] // BLK
    capacity = max(1, 2 * OUT_SLOTS // n_dp)
    rows = -(-bits // 8) * 8
    chunk_slots = 8
    chunks = in_slots // chunk_slots
    sends = n_dp * capacity
    table = (fill.shape[0] // LANES, LANES)
    smem = pltpu.SMEM
    vmem = pl.BlockSpec(memory_space=pltpu.VMEM)
    hbm = pl.BlockSpec(memory_space=pltpu.HBM)
    dma = pltpu.SemaphoreType.DMA
    cot, wg, loss = pl.pallas_call(
        functools.partial(exchange_kernel, n_dp, n_mp, bits, capacity, chunk_slots),
        out_shape=(
            jax.ShapeDtypeStruct((bits, OUT_SLOTS * BLK), BF16),
            jax.ShapeDtypeStruct((bits, 1, width), F32),
            jax.ShapeDtypeStruct((1, LANES), F32),
        ),
        in_specs=[hbm, hbm, hbm, hbm, vmem, vmem],
        out_specs=(vmem, vmem, vmem),
        scratch_shapes=[
            pltpu.VMEM(latents.shape, BF16),
            pltpu.VMEM(table, jnp.int32),
            pltpu.VMEM(table, jnp.int32),
            pltpu.VMEM(table, jnp.int32),
            pltpu.VMEM((in_slots, BLK), F32),
            pltpu.VMEM((in_slots, rows, BLK), F32),
            pltpu.VMEM((in_slots, rows, BLK), F32),
            pltpu.VMEM((chunks, 2 * rows, chunk_slots * BLK), BF16),
            pltpu.VMEM((1, LANES), F32),
            pltpu.VMEM((n_dev, 1, LANES), F32),
            pltpu.VMEM((n_dp, capacity * bits, BLK), BF16),
            pltpu.VMEM((n_dp, capacity * bits, BLK), BF16),
            pltpu.VMEM((sends, bits, BLK), F32),
            pltpu.VMEM((n_dp, in_slots), F32),
            pltpu.VMEM((2, 1, LANES), jnp.int32),
            smem((1, LANES), jnp.int32),
            smem((1, LANES), jnp.int32),
            pltpu.VMEM((bits, 1, width), F32),
            pltpu.VMEM((n_dev, 1, width), F32),
            pltpu.VMEM((1, width), F32),
            pltpu.VMEM((bits, 1, width), F32),
            dma((chunks,)), dma((3,)), dma((2,)), dma(()), dma(()), dma(()), dma((n_dp,)),
            dma(()), dma(()), dma(()), dma(()),
        ],
        compiler_params=pltpu.CompilerParams(
            collective_id=0, has_side_effects=True, vmem_limit_bytes=67043328
        ),
        name="exchange",
    )(fill.reshape(table), target.reshape(table), target_slot.reshape(table), latents, proj_weight,
      proj_bias.reshape(1, bits))
    step = 1024
    grad, wg = pl.pallas_call(
        finish_kernel,
        out_shape=(
            jax.ShapeDtypeStruct((OUT_SLOTS * BLK, width), BF16),
            jax.ShapeDtypeStruct((bits, width), F32),
        ),
        grid=(OUT_SLOTS * BLK // step,),
        in_specs=[
            pl.BlockSpec((bits, step), lambda g: (0, g)),
            pl.BlockSpec((bits, width), lambda g: (0, 0)),
            pl.BlockSpec((bits, 1, width), lambda g: (0, 0, 0)),
        ],
        out_specs=(
            pl.BlockSpec((step, width), lambda g: (g, 0)),
            pl.BlockSpec((bits, width), lambda g: (0, 0)),
        ),
        name="finish",
    )(cot, proj_weight, wg)
    return grad, wg, loss[0, 0]


def solution(mesh):
    placed = (P(("dp", "mp"), None), P(), P(), P(), P(), P())
    return jax.shard_map(
        local,
        mesh=mesh,
        in_specs=placed,
        out_specs=(P(("dp", "mp"), None), P(), P()),
        check_vma=False,
    )
```

time: 39.4 us -> 30.9 us (0.78)
  local copies, waits for them, and re-layouts: 7.29 us -> 0 us
  other arithmetic: 2.97 us -> 0 us
  Pallas kernels: 26.2 us -> 28.1 us
    unnamed x7 -> x0, local copies, waits for them, and re-layouts: 3.49 us -> none
    reduce_sum x5 -> x0, other arithmetic: 2.86 us -> none  [the longest x1 1.34 us: local(): count = jnp.sum(fill).astype(F32).reshape(1)]
    pallas_call x1, Pallas kernels: 21.9 us -> 24.3 us  [local(): pl.pallas_call(functools.partial(exchange_kernel, n_dp, n_mp, bits, capac...]
    reshape x4 -> x0, local copies, waits for them, and re-layouts: 2.3 us -> none  [the longest x1 0.78 us: routing(): target_slot.reshape(shape)]
    dynamic_slice x2 -> x0, local copies, waits for them, and re-layouts: 0.78 us -> none  [the longest x1 0.77 us: local(): lax.dynamic_slice(fill, ((own_dp * n_mp + own_mp) * in_slots,), (in_slots,))]
    pad x1 -> x0, local copies, waits for them, and re-layouts: 0.71 us -> none  [local(): w_pad = jnp.pad(proj_weight, ((0, rows - bits), (0, 0)))]
    pallas_call x1, Pallas kernels: 4.32 us -> 3.88 us  [local(): pl.pallas_call(finish_kernel, out_shape=(jax.ShapeDtypeStruct((OUT_SLOTS...]
where the time goes in v2:
time: 30.9 us; the launch traced here: 30.5 us
  Pallas kernels  28.1 us (91%)
  between operations  2.39 us (8%)
    pallas_call x1, Pallas kernels, local(): pl.pallas_call(functools.partial(exchange_kernel, n_dp, n_mp, bits, capac...  24.3 us
    pallas_call x1, Pallas kernels, local(): pl.pallas_call(finish_kernel, out_shape=(jax.ShapeDtypeStruct((OUT_SLOTS...  3.88 us

profile of v2, /device:TPU:0, one launch (start us, length us, event | category | flops | bytes accessed | tf_op | source)
XLA Modules:
  0.0 30.5 jit_solution(14193075485191605897)
XLA Ops:
  0.6 24.3 %exchange.1 = (bf16[18,4096]{1,0:T(8,128)(2,1)}, f32[18,1,256]{2,1,0:T(1,128)}, f32[1,128]{1,0:T(1,128)}) custom-call(s32[16,128]{1,0:T(8,128)} %bitcast.6, s32[16,128]{1,0:T(8,128)} %bitcast.7, s32[16,128]{1,0:T(8,128)} %bitcast.8, bf16[8192,256]{1,0:T(8,128)(2,1)} %x_hbm.1, bf16[18,256]{1,0:T(8,128)(2,1)} %w_ref.3, f32[1,18]{1,0:T(1,128)} %bitcast.9), custom_call_target="tpu_custom_call" | custom-call | tf_op jit(solution)/shard_map/exchange/pallas_call | solution.py:305
  24.9 3.9 %finish.1 = (bf16[4096,256]{1,0:T(8,128)(2,1)}, f32[18,256]{1,0:T(8,128)}) custom-call(bf16[18,4096]{1,0:T(8,128)(2,1)} %get-tuple-element.8.cot_ref, bf16[18,256]{1,0:T(8,128)(2,1)} %w_ref.3, f32[18,1,256]{2,1,0:T(1,128)} %get-tuple-element.9.wg_ref), custom_call_target="tpu_custom_call" | custom-call | tf_op jit(solution)/shard_map/finish/pallas_call | solution.py:346

commit v3 on v2

v3 whole, which is shorter than its diff:
```python
import functools

import jax
import jax.numpy as jnp
from jax import lax
from jax.experimental import pallas as pl
from jax.experimental.pallas import tpu as pltpu
from jax.sharding import PartitionSpec as P

BLK = 128
OUT_SLOTS = 32
LANES = 128
F32 = jnp.float32
BF16 = jnp.bfloat16
MESH = pl.DeviceIdType.MESH

sharpness = 2.0


def wait_bytes(ref, sem):
    pltpu.make_async_copy(ref, ref, sem).wait()


def to_column(row, rows):
    shape = (rows, row.shape[1])
    diagonal = lax.broadcasted_iota(jnp.int32, shape, 0) == lax.broadcasted_iota(jnp.int32, shape, 1)
    return jnp.sum(jnp.where(diagonal, jnp.broadcast_to(row, shape), 0.0), axis=1, keepdims=True)


def to_row(column):
    shape = (column.shape[0], LANES)
    diagonal = lax.broadcasted_iota(jnp.int32, shape, 0) == lax.broadcasted_iota(jnp.int32, shape, 1)
    return jnp.sum(jnp.where(diagonal, jnp.broadcast_to(column, shape), 0.0), axis=0, keepdims=True)


def slot_row(ref, index, in_slots):
    per = LANES // in_slots
    line = ref[pl.ds(lax.div(index, per), 1), :].astype(F32)
    which = lax.rem(index, per)
    row = line[:, :in_slots]
    for i in range(1, per):
        row = jnp.where(which == i, line[:, i * in_slots:(i + 1) * in_slots], row)
    return row


def exchange_kernel(
    n_dp, n_mp, capacity, chunk_slots,
    fill_hbm, target_hbm, slot_hbm, x_hbm, w_ref, bias_ref,
    cot_ref, wg_ref, loss_ref,
    xbuf, fill_ref, target_ref, slot_ref, mask_ref, out_mask, scaled_ref, stat_own, stat_all,
    send_buf, land, mine_ref, index_vec, chosen_ref, order_ref, wg_own, wg_parts, wg_row, wg_all,
    x_sem, small_sem, index_sem, stat_send, stat_recv, cot_send, cot_recv, part_send, part_recv, row_send, row_recv,
):
    n_dev = n_dp * n_mp
    in_slots, rows, _ = scaled_ref.shape
    bits, width = w_ref.shape
    out_slots = cot_ref.shape[0]
    chunk = chunk_slots * BLK
    chunks = xbuf.shape[0] // chunk
    own_dp = lax.axis_index("dp")
    own_mp = lax.axis_index("mp")
    own = own_dp * n_mp + own_mp

    def device(i):
        return {"dp": lax.div(i, n_mp), "mp": lax.rem(i, n_mp)}

    def x_copy(c):
        part = pl.ds(c * chunk, chunk)
        return pltpu.make_async_copy(x_hbm.at[part], xbuf.at[part], x_sem.at[c])

    small = [
        pltpu.make_async_copy(src, dst, small_sem.at[i])
        for i, (src, dst) in enumerate(((fill_hbm, fill_ref), (target_hbm, target_ref), (slot_hbm, slot_ref)))
    ]
    for copy in small:
        copy.start()
    for c in range(chunks):
        x_copy(c).start()

    barrier = pltpu.get_barrier_semaphore()

    @pl.loop(1, n_dev)
    def _(off):
        pl.semaphore_signal(barrier, inc=1, device_id=device(lax.rem(own + off, n_dev)), device_id_type=MESH)

    bias = to_column(bias_ref[...], rows)
    w = w_ref[...]
    w = jnp.concatenate([w.astype(F32), jnp.zeros((rows - bits, width), F32)], axis=0).astype(BF16)
    live_row = (lax.broadcasted_iota(jnp.int32, (rows, 1), 0) < bits).astype(F32)
    lanes = lax.broadcasted_iota(jnp.int32, (1, LANES), 1)
    for copy in small:
        copy.wait()

    target_row = slot_row(target_ref, own, in_slots)
    target_col = to_column(target_row, in_slots)
    before = lax.broadcasted_iota(jnp.int32, (in_slots, in_slots), 1) < lax.broadcasted_iota(
        jnp.int32, (in_slots, in_slots), 0
    )
    rank = jnp.sum(jnp.where((target_col == target_row) & before, 1.0, 0.0), axis=1, keepdims=True)
    position = jnp.where(target_col >= 0.0, target_col * float(capacity) + rank, -1.0)
    send_lane = lax.broadcasted_iota(jnp.int32, (in_slots, LANES), 1).astype(F32)
    send_slot = lax.broadcasted_iota(jnp.int32, (in_slots, LANES), 0).astype(F32)
    chosen = jnp.sum(jnp.where(position == send_lane, send_slot, 0.0), axis=0, keepdims=True)
    index_vec[0] = chosen.astype(jnp.int32)
    choose = pltpu.make_async_copy(index_vec.at[0], chosen_ref, index_sem.at[0])
    choose.start()

    fill_col = to_column(slot_row(fill_ref, own, in_slots), in_slots)
    token = lax.broadcasted_iota(jnp.int32, (in_slots, BLK), 1).astype(F32)
    mask_ref[...] = (token < fill_col).astype(F32)
    fills = fill_ref[...].astype(F32)
    count = jnp.sum(jnp.sum(fills, axis=0, keepdims=True), axis=1, keepdims=True)

    @pl.loop(0, chunks)
    def _(c):
        x_copy(c).wait()
        x = xbuf[pl.ds(pl.multiple_of(c * chunk, chunk), chunk), :]
        logits = lax.dot_general(w, x, (((1,), (1,)), ((), ())), preferred_element_type=F32) + bias
        scaled = sharpness * logits
        for i in range(chunk_slots):
            scaled_ref[c * chunk_slots + i] = scaled[:, i * BLK:(i + 1) * BLK]

    choose.wait()
    pl.semaphore_wait(barrier, n_dev - 1)

    @pl.loop(1, n_dp + 1)
    def _(off):
        peer = lax.rem(own_dp + off, n_dp)

        def pack(ref):
            for k in range(capacity):
                slot = jnp.clip(chosen_ref[0, peer * capacity + k], 0, in_slots - 1)
                ref[peer, k * bits:(k + 1) * bits, :] = scaled_ref[slot][:bits]

        @pl.when(off == n_dp)
        def _():
            pack(land)

        @pl.when(off < n_dp)
        def _():
            pack(send_buf)
            pltpu.make_async_remote_copy(
                src_ref=send_buf.at[peer], dst_ref=land.at[own_dp], send_sem=cot_send, recv_sem=cot_recv,
                device_id={"dp": peer, "mp": own_mp}, device_id_type=MESH,
            ).start()

    def statistics(c, carry):
        bit_acc, ent_acc, both = carry
        x = xbuf[pl.ds(pl.multiple_of(c * chunk, chunk), chunk), :]
        scaled = jnp.concatenate([scaled_ref[c * chunk_slots + i] for i in range(chunk_slots)], axis=1)
        mask = jnp.concatenate(
            [mask_ref[pl.ds(c * chunk_slots + i, 1), :] for i in range(chunk_slots)], axis=1
        )
        size = jnp.abs(scaled)
        e = jnp.exp(-size)
        u = 1.0 + e
        r = 1.0 / u
        er = e * r
        prob = jnp.where(scaled >= 0, r, er) * mask
        ent = (jnp.log(u) + (e - (u - 1.0)) * r + size * er) * mask
        second = 2.0 * (er * r * mask)
        first = -(scaled * second)
        rounded = jnp.concatenate([first, second], axis=0).astype(BF16)
        both = both + jnp.dot(rounded, x, preferred_element_type=F32)
        for i in range(chunk_slots):
            cols = slice(i * BLK, (i + 1) * BLK)
            bit_acc = bit_acc + prob[:, cols]
            ent_acc = ent_acc + ent[:, cols]
        return bit_acc, ent_acc, both

    zero = jnp.zeros((rows, BLK), F32)
    bit_acc, ent_acc, both = lax.fori_loop(
        0, chunks, statistics, (zero, zero, jnp.zeros((2 * rows, width), F32))
    )
    bit_row = to_row(jnp.sum(bit_acc, axis=1, keepdims=True) * live_row)
    ent_sum = jnp.sum(jnp.sum(ent_acc * live_row, axis=1, keepdims=True), axis=0, keepdims=True)
    stat = jnp.where(lanes == LANES - 1, jnp.broadcast_to(ent_sum, (1, LANES)), bit_row)
    stat_own[...] = stat
    stat_all[own] = stat
    for b in range(bits):
        wg_own[b, 0:1, :] = both[b:b + 1]
        wg_own[b, 1:2, :] = both[rows + b:rows + b + 1]
    wg_parts[own] = wg_own[jnp.minimum(own, bits - 1)]

    @pl.loop(1, n_dev)
    def _(off):
        pltpu.make_async_remote_copy(
            src_ref=stat_own, dst_ref=stat_all.at[own], send_sem=stat_send, recv_sem=stat_recv,
            device_id=device(lax.rem(own + off, n_dev)), device_id_type=MESH,
        ).start()

    @pl.loop(0, bits)
    def _(b):
        @pl.when(b != own)
        def _():
            pltpu.make_async_remote_copy(
                src_ref=wg_own.at[b], dst_ref=wg_parts.at[own], send_sem=part_send, recv_sem=part_recv,
                device_id=device(b), device_id_type=MESH,
            ).start()

    for d in range(n_dp):
        mine_ref[d:d + 1, :] = jnp.where(slot_row(target_ref, d * n_mp + own_mp, in_slots) == own_dp.astype(F32), 1.0, 0.0)
    mine = mine_ref[...]
    later = lax.broadcasted_iota(jnp.int32, (in_slots, in_slots), 0) < lax.broadcasted_iota(
        jnp.int32, (in_slots, in_slots), 1
    )
    ranks = jnp.dot(mine.astype(BF16), later.astype(F32).astype(BF16), preferred_element_type=F32)
    out_index = lax.broadcasted_iota(jnp.int32, (out_slots, in_slots), 0).astype(F32)
    gathered = jnp.zeros((out_slots, in_slots), F32)
    out_fill = jnp.zeros((out_slots, in_slots), F32)
    for d in range(n_dp):
        taken = (out_index == slot_row(slot_ref, d * n_mp + own_mp, in_slots)) & (mine[d:d + 1] > 0.0)
        gathered = gathered + jnp.where(taken, float(d * capacity) + ranks[d:d + 1], 0.0)
        out_fill = out_fill + jnp.where(taken, slot_row(fill_ref, d * n_mp + own_mp, in_slots), 0.0)
    index_vec[1] = to_row(jnp.sum(gathered, axis=1, keepdims=True)).astype(jnp.int32)
    ordering = pltpu.make_async_copy(index_vec.at[1], order_ref, index_sem.at[1])
    ordering.start()
    out_token = lax.broadcasted_iota(jnp.int32, (out_slots, BLK), 1).astype(F32)
    out_mask[...] = (out_token < jnp.sum(out_fill, axis=1, keepdims=True)).astype(F32)

    wait_bytes(stat_all.at[pl.ds(0, n_dev - 1)], stat_recv)
    total = jnp.sum(stat_all[...], axis=0)
    marginal_c = to_column(total, rows) / count
    log_odds = jnp.log(1.0 - marginal_c) - jnp.log(marginal_c)
    log_odds = jnp.where(live_row > 0, log_odds, 0.0)

    @pl.when(own < bits)
    def _():
        row_index = lax.broadcasted_iota(jnp.int32, (rows, 1), 0)
        own_odds = jnp.sum(jnp.where(row_index == own, log_odds, 0.0), axis=0, keepdims=True)
        wait_bytes(wg_parts.at[pl.ds(0, n_dev - 1)], part_recv)
        parts = jnp.sum(wg_parts[...], axis=0)
        row = (parts[0:1] - parts[1:2] * own_odds) / jnp.sqrt(count)
        wg_row[...] = row
        wg_all[own] = row

        @pl.loop(1, n_dev)
        def _(off):
            pltpu.make_async_remote_copy(
                src_ref=wg_row, dst_ref=wg_all.at[own], send_sem=row_send, recv_sem=row_recv,
                device_id=device(lax.rem(own + off, n_dev)), device_id_type=MESH,
            ).start()

    marginal = total / count
    inside = lanes < bits
    safe = jnp.where(inside, marginal, 0.5)
    plain = safe * jnp.log(safe) + (1.0 - safe) * jnp.log(1.0 - safe)
    neg_codebook = jnp.sum(jnp.where(inside, plain, 0.0), axis=1, keepdims=True)
    ent_all = jnp.sum(jnp.where(lanes == LANES - 1, total, 0.0), axis=1, keepdims=True)
    loss_ref[...] = jnp.broadcast_to(ent_all / count + neg_codebook, (1, LANES))

    ordering.wait()
    wait_bytes(land.at[pl.ds(0, n_dp - 1)], cot_recv)
    odds = log_odds[:bits]
    for k in range(out_slots):
        at = jnp.clip(order_ref[0, k], 0, n_dp * capacity - 1)
        scaled = land[lax.div(at, capacity), pl.ds(lax.rem(at, capacity) * bits, bits), :]
        e = jnp.exp(-jnp.abs(scaled))
        r = 1.0 / (1.0 + e)
        second = 2.0 * (e * r * r * out_mask[k:k + 1, :])
        cot_ref[k] = (-(scaled * second) - second * odds).astype(BF16)

    @pl.when(own < bits)
    def _():
        wait_bytes(wg_all.at[pl.ds(0, bits - 1)], row_recv)
        wait_bytes(wg_own.at[pl.ds(0, bits - 1)], part_send)
        for _ in range(n_dev - 1):
            wait_bytes(wg_row, row_send)

    @pl.when(own >= bits)
    def _():
        wait_bytes(wg_all.at[pl.ds(0, bits)], row_recv)
        wait_bytes(wg_own.at[pl.ds(0, bits)], part_send)

    wg_ref[...] = wg_all[...]
    wait_bytes(stat_all.at[pl.ds(0, n_dev - 1)], stat_send)
    wait_bytes(send_buf.at[pl.ds(0, n_dp - 1)], cot_send)


def local(latents, proj_weight, proj_bias, fill, target, target_slot):
    n_dp = lax.axis_size("dp")
    n_mp = lax.axis_size("mp")
    n_dev = n_dp * n_mp
    width = latents.shape[1]
    bits = proj_weight.shape[0]
    in_slots = latents.shape[0] // BLK
    capacity = max(1, 2 * OUT_SLOTS // n_dp)
    rows = -(-bits // 8) * 8
    chunk_slots = 8
    chunks = in_slots // chunk_slots
    table = (fill.shape[0] // LANES, LANES)
    smem = pltpu.SMEM
    vmem = pl.BlockSpec(memory_space=pltpu.VMEM)
    hbm = pl.BlockSpec(memory_space=pltpu.HBM)
    dma = pltpu.SemaphoreType.DMA
    cot, wg, loss = pl.pallas_call(
        functools.partial(exchange_kernel, n_dp, n_mp, capacity, chunk_slots),
        out_shape=(
            jax.ShapeDtypeStruct((OUT_SLOTS, bits, BLK), BF16),
            jax.ShapeDtypeStruct((bits, 1, width), F32),
            jax.ShapeDtypeStruct((1, LANES), F32),
        ),
        in_specs=[hbm, hbm, hbm, hbm, vmem, vmem],
        out_specs=(vmem, vmem, vmem),
        scratch_shapes=[
            pltpu.VMEM(latents.shape, BF16),
            pltpu.VMEM(table, jnp.int32),
            pltpu.VMEM(table, jnp.int32),
            pltpu.VMEM(table, jnp.int32),
            pltpu.VMEM((in_slots, BLK), F32),
            pltpu.VMEM((OUT_SLOTS, BLK), F32),
            pltpu.VMEM((in_slots, rows, BLK), F32),
            pltpu.VMEM((1, LANES), F32),
            pltpu.VMEM((n_dev, 1, LANES), F32),
            pltpu.VMEM((n_dp, capacity * bits, BLK), F32),
            pltpu.VMEM((n_dp, capacity * bits, BLK), F32),
            pltpu.VMEM((n_dp, in_slots), F32),
            pltpu.VMEM((2, 1, LANES), jnp.int32),
            smem((1, LANES), jnp.int32),
            smem((1, LANES), jnp.int32),
            pltpu.VMEM((bits, 2, width), F32),
            pltpu.VMEM((n_dev, 2, width), F32),
            pltpu.VMEM((1, width), F32),
            pltpu.VMEM((bits, 1, width), F32),
            dma((chunks,)), dma((3,)), dma((2,)), dma(()), dma(()), dma(()), dma(()),
            dma(()), dma(()), dma(()), dma(()),
        ],
        compiler_params=pltpu.CompilerParams(
            collective_id=0, has_side_effects=True, vmem_limit_bytes=67043328
        ),
        name="exchange",
    )(fill.reshape(table), target.reshape(table), target_slot.reshape(table), latents, proj_weight,
      proj_bias.reshape(1, bits))
    grad = jnp.einsum("nbk,bd->nkd", cot, proj_weight, preferred_element_type=F32).astype(BF16)
    return grad.reshape(-1, width), wg.reshape(bits, width), loss[0, 0]


def solution(mesh):
    placed = (P(("dp", "mp"), None), P(), P(), P(), P(), P())
    return jax.shard_map(
        local,
        mesh=mesh,
        in_specs=placed,
        out_specs=(P(("dp", "mp"), None), P(), P()),
        check_vma=False,
    )
```

time: 30.9 us -> 36.4 us (1.18)
  matrix products: 0 us -> 3.01 us
  local copies, waits for them, and re-layouts: 0 us -> 1.33 us
  Pallas kernels: 28.1 us -> 29.4 us
    dot_general x0 -> x1, matrix products: none -> 3.01 us  [local(): jnp.einsum('nbk,bd->nkd', cot, proj_weight, preferred_element_type=F32)]
    unnamed x0 -> x1, local copies, waits for them, and re-layouts: none -> 1.33 us
    pallas_call x2 -> x1, Pallas kernels: 28.1 us -> 29.4 us  [local(): pl.pallas_call(functools.partial(exchange_kernel, n_dp, n_mp, capacity, c...]
where the time goes in v3:
time: 36.4 us; the launch traced here: 36.2 us
  Pallas kernels  29.4 us (81%)
  matrix products  3.01 us (8%)
  between operations  2.4 us (7%)
  local copies, waits for them, and re-layouts  1.33 us (4%)
    pallas_call x1, Pallas kernels, local(): pl.pallas_call(functools.partial(exchange_kernel, n_dp, n_mp, capacity, c...  29.4 us
    dot_general x1, matrix products, local(): jnp.einsum('nbk,bd->nkd', cot, proj_weight, preferred_element_type=F32)  3.01 us
    unnamed x1, local copies, waits for them, and re-layouts  1.33 us

profile of v3, /device:TPU:0, one launch (start us, length us, event | category | flops | bytes accessed | tf_op | source)
XLA Modules:
  0.0 36.2 jit_solution(6672584760738699944)
XLA Ops:
  0.6 29.4 %exchange.1 = (bf16[32,18,128]{2,1,0:T(8,128)(2,1)}, f32[18,1,256]{2,1,0:T(1,128)}, f32[1,128]{1,0:T(1,128)}) custom-call(s32[16,128]{1,0:T(8,128)} %bitcast.16, s32[16,128]{1,0:T(8,128)} %bitcast.17, s32[16,128]{1,0:T(8,128)} %bitcast.18, bf16[8192,256]{1,0:T(8,128)(2,1)} %x_hbm.1, bf16[18,256]{1,0:T(8,128)(2,1)} %w_ref.1, f32[1,18]{1,0:T(1,128)} %bitcast.19), custom_call_target="tpu_custom_call" | custom-call | tf_op jit(solution)/shard_map/exchange/pallas_call | solution.py:296
  30.1 3.0 %convolution_convert_fusion = bf16[32,128,256]{2,1,0:T(8,128)(2,1)} fusion(bf16[32,18,128]{2,1,0:T(8,128)(2,1)} %get-tuple-element.6, bf16[18,256]{1,0:T(8,128)(2,1)} %w_ref.1), kind=kOutput, calls=%fused_computation | convolution fusion | flops 38797312 | bytes 2253824 | tf_op jit(solution)/shard_map/nbk,bd->nkd/dot_general | solution.py:334
  33.1 1.3 %copy.11 = f32[18,1,256]{2,0,1:T(8,128)} copy(f32[18,1,256]{2,1,0:T(1,128)} %get-tuple-element.7) | data formatting | bytes 36864

commit v4 on v3

v4 whole, which is shorter than its diff:
```python
import functools

import jax
import jax.numpy as jnp
from jax import lax
from jax.experimental import pallas as pl
from jax.experimental.pallas import tpu as pltpu
from jax.sharding import PartitionSpec as P

BLK = 128
OUT_SLOTS = 32
LANES = 128
F32 = jnp.float32
BF16 = jnp.bfloat16
MESH = pl.DeviceIdType.MESH

sharpness = 2.0


def wait_bytes(ref, sem):
    pltpu.make_async_copy(ref, ref, sem).wait()


def to_column(row, rows):
    shape = (rows, row.shape[1])
    diagonal = lax.broadcasted_iota(jnp.int32, shape, 0) == lax.broadcasted_iota(jnp.int32, shape, 1)
    return jnp.sum(jnp.where(diagonal, jnp.broadcast_to(row, shape), 0.0), axis=1, keepdims=True)


def to_row(column):
    shape = (column.shape[0], LANES)
    diagonal = lax.broadcasted_iota(jnp.int32, shape, 0) == lax.broadcasted_iota(jnp.int32, shape, 1)
    return jnp.sum(jnp.where(diagonal, jnp.broadcast_to(column, shape), 0.0), axis=0, keepdims=True)


def slot_row(ref, index, in_slots):
    per = LANES // in_slots
    line = ref[pl.ds(lax.div(index, per), 1), :].astype(F32)
    which = lax.rem(index, per)
    row = line[:, :in_slots]
    for i in range(1, per):
        row = jnp.where(which == i, line[:, i * in_slots:(i + 1) * in_slots], row)
    return row


def exchange_kernel(
    n_dp, n_mp, capacity, chunk_slots,
    fill_hbm, target_hbm, slot_hbm, x_hbm, w_ref, bias_ref,
    cot_ref, wg_ref, loss_ref,
    xbuf, fill_ref, target_ref, slot_ref, mask_ref, first_ref, second_ref, dp_own, dp_all, mp_own, mp_all,
    row_own, row_all, send_buf, land, landed, mine_ref, index_vec, chosen_ref, order_ref,
    x_sem, small_sem, index_sem, dp_send, dp_recv, mp_send, mp_recv, cot_send, cot_recv, row_send, row_recv,
):
    in_slots, rows, _ = first_ref.shape
    depth = dp_own.shape[1]
    bits, width = w_ref.shape
    out_slots = cot_ref.shape[0]
    chunk = chunk_slots * BLK
    chunks = xbuf.shape[0] // chunk
    own_dp = lax.axis_index("dp")
    own_mp = lax.axis_index("mp")
    own = own_dp * n_mp + own_mp
    piece = -(-bits // n_dp)

    def dp_peer(off):
        return {"dp": lax.rem(own_dp + off, n_dp), "mp": own_mp}

    def mp_peer(off):
        return {"dp": own_dp, "mp": lax.rem(own_mp + off, n_mp)}

    def x_copy(c):
        part = pl.ds(c * chunk, chunk)
        return pltpu.make_async_copy(x_hbm.at[part], xbuf.at[part], x_sem.at[c])

    small = [
        pltpu.make_async_copy(src, dst, small_sem.at[i])
        for i, (src, dst) in enumerate(((fill_hbm, fill_ref), (target_hbm, target_ref), (slot_hbm, slot_ref)))
    ]
    for copy in small:
        copy.start()
    for c in range(chunks):
        x_copy(c).start()

    barrier = pltpu.get_barrier_semaphore()

    @pl.loop(1, n_dp)
    def _(off):
        pl.semaphore_signal(barrier, inc=1, device_id=dp_peer(off), device_id_type=MESH)

    @pl.loop(1, n_mp)
    def _(off):
        pl.semaphore_signal(barrier, inc=1, device_id=mp_peer(off), device_id_type=MESH)

    bias = to_column(bias_ref[...], rows)
    w = w_ref[...]
    w = jnp.concatenate([w.astype(F32), jnp.zeros((rows - bits, width), F32)], axis=0).astype(BF16)
    live_row = (lax.broadcasted_iota(jnp.int32, (rows, 1), 0) < bits).astype(F32)
    lanes = lax.broadcasted_iota(jnp.int32, (1, LANES), 1)
    for copy in small:
        copy.wait()

    target_row = slot_row(target_ref, own, in_slots)
    target_col = to_column(target_row, in_slots)
    before = lax.broadcasted_iota(jnp.int32, (in_slots, in_slots), 1) < lax.broadcasted_iota(
        jnp.int32, (in_slots, in_slots), 0
    )
    rank = jnp.sum(jnp.where((target_col == target_row) & before, 1.0, 0.0), axis=1, keepdims=True)
    position = jnp.where(target_col >= 0.0, target_col * float(capacity) + rank, -1.0)
    send_lane = lax.broadcasted_iota(jnp.int32, (in_slots, LANES), 1).astype(F32)
    send_slot = lax.broadcasted_iota(jnp.int32, (in_slots, LANES), 0).astype(F32)
    chosen = jnp.sum(jnp.where(position == send_lane, send_slot, 0.0), axis=0, keepdims=True)
    index_vec[0] = chosen.astype(jnp.int32)
    choose = pltpu.make_async_copy(index_vec.at[0], chosen_ref, index_sem.at[0])
    choose.start()

    fill_col = to_column(slot_row(fill_ref, own, in_slots), in_slots)
    token = lax.broadcasted_iota(jnp.int32, (in_slots, BLK), 1).astype(F32)
    mask_ref[...] = (token < fill_col).astype(F32)
    fills = fill_ref[...].astype(F32)
    count = jnp.sum(jnp.sum(fills, axis=0, keepdims=True), axis=1, keepdims=True)

    def statistics(c, carry):
        bit_acc, ent_acc, both = carry
        x_copy(c).wait()
        x = xbuf[pl.ds(pl.multiple_of(c * chunk, chunk), chunk), :]
        logits = lax.dot_general(w, x, (((1,), (1,)), ((), ())), preferred_element_type=F32) + bias
        scaled = sharpness * logits
        mask = jnp.concatenate(
            [mask_ref[pl.ds(c * chunk_slots + i, 1), :] for i in range(chunk_slots)], axis=1
        )
        size = jnp.abs(scaled)
        e = jnp.exp(-size)
        u = 1.0 + e
        r = 1.0 / u
        er = e * r
        prob = jnp.where(scaled >= 0, r, er) * mask
        ent = (jnp.log(u) + (e - (u - 1.0)) * r + size * er) * mask
        second = 2.0 * (er * r * mask)
        first = -(scaled * second)
        rounded = jnp.concatenate([first, second], axis=0).astype(BF16)
        both = both + jnp.dot(rounded, x, preferred_element_type=F32)
        for i in range(chunk_slots):
            cols = slice(i * BLK, (i + 1) * BLK)
            first_ref[c * chunk_slots + i] = first[:, cols]
            second_ref[c * chunk_slots + i] = second[:, cols]
            bit_acc = bit_acc + prob[:, cols]
            ent_acc = ent_acc + ent[:, cols]
        return bit_acc, ent_acc, both

    zero = jnp.zeros((rows, BLK), F32)
    bit_acc, ent_acc, both = lax.fori_loop(
        0, chunks, statistics, (zero, zero, jnp.zeros((2 * rows, width), F32))
    )
    bit_row = to_row(jnp.sum(bit_acc, axis=1, keepdims=True) * live_row)
    ent_sum = jnp.sum(jnp.sum(ent_acc * live_row, axis=1, keepdims=True), axis=0, keepdims=True)
    stat = jnp.where(lanes == LANES - 1, jnp.broadcast_to(ent_sum, (1, LANES)), bit_row)
    stat = jnp.concatenate([stat, jnp.zeros((1, width - LANES), F32)], axis=1)
    blank = jnp.zeros((1, width), F32)
    for d in range(n_dp):
        mine_bits = [b if b < bits else None for b in range(d * piece, (d + 1) * piece)]
        lines = [blank if b is None else both[b:b + 1] for b in mine_bits]
        lines += [blank if b is None else both[rows + b:rows + b + 1] for b in mine_bits]
        lines += [stat] + [blank] * (depth - 2 * piece - 1)
        dp_own[d] = jnp.concatenate(lines, axis=0)
    dp_all[own_dp] = dp_own[own_dp]
    pl.semaphore_wait(barrier, n_dp + n_mp - 2)

    @pl.loop(1, n_dp)
    def _(off):
        pltpu.make_async_remote_copy(
            src_ref=dp_own.at[lax.rem(own_dp + off, n_dp)], dst_ref=dp_all.at[own_dp],
            send_sem=dp_send, recv_sem=dp_recv, device_id=dp_peer(off), device_id_type=MESH,
        ).start()

    for d in range(n_dp):
        mine_ref[d:d + 1, :] = jnp.where(slot_row(target_ref, d * n_mp + own_mp, in_slots) == own_dp.astype(F32), 1.0, 0.0)
    mine = mine_ref[...]
    later = lax.broadcasted_iota(jnp.int32, (in_slots, in_slots), 0) < lax.broadcasted_iota(
        jnp.int32, (in_slots, in_slots), 1
    )
    ranks = jnp.dot(mine.astype(BF16), later.astype(F32).astype(BF16), preferred_element_type=F32)
    out_index = lax.broadcasted_iota(jnp.int32, (out_slots, in_slots), 0).astype(F32)
    gathered = jnp.zeros((out_slots, in_slots), F32)
    for d in range(n_dp):
        taken = (out_index == slot_row(slot_ref, d * n_mp + own_mp, in_slots)) & (mine[d:d + 1] > 0.0)
        gathered = gathered + jnp.where(taken, float(d * capacity) + ranks[d:d + 1], 0.0)
    index_vec[1] = to_row(jnp.sum(gathered, axis=1, keepdims=True)).astype(jnp.int32)
    ordering = pltpu.make_async_copy(index_vec.at[1], order_ref, index_sem.at[1])
    ordering.start()
    wait_bytes(dp_all.at[pl.ds(0, n_dp - 1)], dp_recv)
    column_sum = jnp.sum(dp_all[...], axis=0)
    mp_own[...] = column_sum
    mp_all[own_mp] = column_sum

    @pl.loop(1, n_mp)
    def _(off):
        pltpu.make_async_remote_copy(
            src_ref=mp_own, dst_ref=mp_all.at[own_mp],
            send_sem=mp_send, recv_sem=mp_recv, device_id=mp_peer(off), device_id_type=MESH,
        ).start()

    choose.wait()
    wait_bytes(mp_all.at[pl.ds(0, n_mp - 1)], mp_recv)
    sums = jnp.sum(mp_all[...], axis=0)
    total = sums[2 * piece:2 * piece + 1, :LANES]
    marginal_c = to_column(total, rows) / count
    log_odds = jnp.log(1.0 - marginal_c) - jnp.log(marginal_c)
    log_odds = jnp.where(live_row > 0, log_odds, 0.0)

    row_index = lax.broadcasted_iota(jnp.int32, (rows, 1), 0)
    lines = []
    for i in range(piece):
        odds = jnp.sum(jnp.where(row_index == own_dp * piece + i, log_odds, 0.0), axis=0, keepdims=True)
        lines.append((sums[i:i + 1] - sums[piece + i:piece + i + 1] * odds) / jnp.sqrt(count))
    finished = jnp.concatenate(lines + [blank] * (row_own.shape[0] - piece), axis=0)
    row_own[...] = finished
    row_all[own_dp] = finished

    @pl.loop(1, n_dp)
    def _(off):
        pltpu.make_async_remote_copy(
            src_ref=row_own, dst_ref=row_all.at[own_dp],
            send_sem=row_send, recv_sem=row_recv, device_id=dp_peer(off), device_id_type=MESH,
        ).start()

    @pl.loop(1, n_dp + 1)
    def _(off):
        peer = lax.rem(own_dp + off, n_dp)
        blocks = []
        for k in range(capacity):
            slot = jnp.clip(chosen_ref[0, peer * capacity + k], 0, in_slots - 1)
            blocks.append((first_ref[slot] - second_ref[slot] * log_odds)[:bits])
        packed = jnp.concatenate(blocks, axis=0).astype(BF16)

        @pl.when(off == n_dp)
        def _():
            land[own_dp] = packed

        @pl.when(off < n_dp)
        def _():
            send_buf[peer] = packed
            pltpu.make_async_remote_copy(
                src_ref=send_buf.at[peer], dst_ref=land.at[own_dp], send_sem=cot_send, recv_sem=cot_recv.at[own_dp],
                device_id=dp_peer(off), device_id_type=MESH,
            ).start()

    marginal = total / count
    inside = lanes < bits
    safe = jnp.where(inside, marginal, 0.5)
    plain = safe * jnp.log(safe) + (1.0 - safe) * jnp.log(1.0 - safe)
    neg_codebook = jnp.sum(jnp.where(inside, plain, 0.0), axis=1, keepdims=True)
    ent_all = jnp.sum(jnp.where(lanes == LANES - 1, total, 0.0), axis=1, keepdims=True)
    loss_ref[...] = jnp.broadcast_to(ent_all / count + neg_codebook, (1, LANES))

    ordering.wait()

    @pl.loop(0, n_dp)
    def _(off):
        src = lax.rem(own_dp + n_dp - off, n_dp)

        @pl.when(off > 0)
        def _():
            wait_bytes(land.at[src], cot_recv.at[src])

        arrived = land[src].astype(F32)
        for k in range(capacity):
            landed[src * capacity + k] = arrived[k * bits:(k + 1) * bits]

    for k in range(out_slots):
        cot_ref[k] = landed[jnp.clip(order_ref[0, k], 0, n_dp * capacity - 1)].astype(BF16)

    wait_bytes(row_all.at[pl.ds(0, n_dp - 1)], row_recv)
    wg_ref[...] = jnp.concatenate([row_all[b // piece, b % piece:b % piece + 1, :] for b in range(bits)], axis=0)
    wait_bytes(dp_own.at[pl.ds(0, n_dp - 1)], dp_send)
    wait_bytes(mp_all.at[pl.ds(0, n_mp - 1)], mp_send)
    wait_bytes(row_all.at[pl.ds(0, n_dp - 1)], row_send)
    wait_bytes(send_buf.at[pl.ds(0, n_dp - 1)], cot_send)


def local(latents, proj_weight, proj_bias, fill, target, target_slot):
    n_dp = lax.axis_size("dp")
    n_mp = lax.axis_size("mp")
    width = latents.shape[1]
    bits = proj_weight.shape[0]
    in_slots = latents.shape[0] // BLK
    capacity = max(1, 2 * OUT_SLOTS // n_dp)
    rows = -(-bits // 8) * 8
    piece = -(-bits // n_dp)
    depth = -(-(2 * piece + 1) // 8) * 8
    row_depth = -(-piece // 8) * 8
    chunk_slots = 8
    chunks = in_slots // chunk_slots
    table = (fill.shape[0] // LANES, LANES)
    smem = pltpu.SMEM
    vmem = pl.BlockSpec(memory_space=pltpu.VMEM)
    hbm = pl.BlockSpec(memory_space=pltpu.HBM)
    dma = pltpu.SemaphoreType.DMA
    cot, wg, loss = pl.pallas_call(
        functools.partial(exchange_kernel, n_dp, n_mp, capacity, chunk_slots),
        out_shape=(
            jax.ShapeDtypeStruct((OUT_SLOTS, bits, BLK), BF16),
            jax.ShapeDtypeStruct((bits, width), F32),
            jax.ShapeDtypeStruct((1, LANES), F32),
        ),
        in_specs=[hbm, hbm, hbm, hbm, vmem, vmem],
        out_specs=(vmem, vmem, vmem),
        scratch_shapes=[
            pltpu.VMEM(latents.shape, BF16),
            pltpu.VMEM(table, jnp.int32),
            pltpu.VMEM(table, jnp.int32),
            pltpu.VMEM(table, jnp.int32),
            pltpu.VMEM((in_slots, BLK), F32),
            pltpu.VMEM((in_slots, rows, BLK), F32),
            pltpu.VMEM((in_slots, rows, BLK), F32),
            pltpu.VMEM((n_dp, depth, width), F32),
            pltpu.VMEM((n_dp, depth, width), F32),
            pltpu.VMEM((depth, width), F32),
            pltpu.VMEM((n_mp, depth, width), F32),
            pltpu.VMEM((row_depth, width), F32),
            pltpu.VMEM((n_dp, row_depth, width), F32),
            pltpu.VMEM((n_dp, capacity * bits, BLK), BF16),
            pltpu.VMEM((n_dp, capacity * bits, BLK), BF16),
            pltpu.VMEM((n_dp * capacity, bits, BLK), F32),
            pltpu.VMEM((n_dp, in_slots), F32),
            pltpu.VMEM((2, 1, LANES), jnp.int32),
            smem((1, LANES), jnp.int32),
            smem((1, LANES), jnp.int32),
            dma((chunks,)), dma((3,)), dma((2,)), dma(()), dma(()), dma(()), dma(()),
            dma(()), dma((n_dp,)), dma(()), dma(()),
        ],
        compiler_params=pltpu.CompilerParams(
            collective_id=0, has_side_effects=True, vmem_limit_bytes=67043328
        ),
        name="exchange",
    )(fill.reshape(table), target.reshape(table), target_slot.reshape(table), latents, proj_weight,
      proj_bias.reshape(1, bits))
    grad = jnp.einsum("nbk,bd->nkd", cot, proj_weight, preferred_element_type=F32).astype(BF16)
    return grad.reshape(-1, width), wg, loss[0, 0]


def solution(mesh):
    placed = (P(("dp", "mp"), None), P(), P(), P(), P(), P())
    return jax.shard_map(
        local,
        mesh=mesh,
        in_specs=placed,
        out_specs=(P(("dp", "mp"), None), P(), P()),
        check_vma=False,
    )
```

time: 36.4 us -> 33.3 us (0.915)
  Pallas kernels: 29.4 us -> 26.3 us
    pallas_call x1, Pallas kernels: 29.4 us -> 26.3 us  [local(): pl.pallas_call(functools.partial(exchange_kernel, n_dp, n_mp, capacity, c...]
where the time goes in v4:
time: 33.3 us; the launch traced here: 33 us
  Pallas kernels  26.3 us (79%)
  matrix products  3.01 us (9%)
  between operations  2.4 us (7%)
  local copies, waits for them, and re-layouts  1.35 us (4%)
    pallas_call x1, Pallas kernels, local(): pl.pallas_call(functools.partial(exchange_kernel, n_dp, n_mp, capacity, c...  26.3 us
    dot_general x1, matrix products, local(): jnp.einsum('nbk,bd->nkd', cot, proj_weight, preferred_element_type=F32)  3.01 us
    unnamed x1, local copies, waits for them, and re-layouts  1.35 us

profile of v4, /device:TPU:0, one launch (start us, length us, event | category | flops | bytes accessed | tf_op | source)
XLA Modules:
  0.0 33.0 jit_solution(8601469521726834554)
XLA Ops:
  0.6 26.3 %exchange.1 = (bf16[32,18,128]{2,1,0:T(8,128)(2,1)}, f32[18,256]{1,0:T(8,128)}, f32[1,128]{1,0:T(1,128)}) custom-call(s32[16,128]{1,0:T(8,128)} %bitcast.12, s32[16,128]{1,0:T(8,128)} %bitcast.13, s32[16,128]{1,0:T(8,128)} %bitcast.14, bf16[8192,256]{1,0:T(8,128)(2,1)} %x_hbm.1, bf16[18,256]{1,0:T(8,128)(2,1)} %w_ref.1, f32[1,18]{1,0:T(1,128)} %bitcast.15), custom_call_target="tpu_custom_call" | custom-call | tf_op jit(solution)/shard_map/exchange/pallas_call | solution.py:298
  26.9 3.0 %convolution_convert_fusion = bf16[32,128,256]{2,1,0:T(8,128)(2,1)} fusion(bf16[32,18,128]{2,1,0:T(8,128)(2,1)} %get-tuple-element.6, bf16[18,256]{1,0:T(8,128)(2,1)} %w_ref.1), kind=kOutput, calls=%fused_computation | convolution fusion | flops 38797312 | bytes 2253824 | tf_op jit(solution)/shard_map/nbk,bd->nkd/dot_general | solution.py:337
  29.9 1.3 %copy.11 = f32[18,256]{1,0:T(8,128)} copy(f32[18,256]{1,0:T(8,128)} %get-tuple-element.13) | data formatting | bytes 36864
